TPU v7x, 128 devices: a whole 4x4x4 slice. The times are simulated.
128 devices in a mesh: expert: 8 (over y, z_lo), shard: 16 (over z_hi, x, core).
Axes of the slice: x: 4, y: 4, z: 4 (z_hi: 2, z_lo: 2; z = z_hi * 2 + z_lo), core: 2. Of those that a mesh axis runs over, the one named last changes fastest.
Arguments:
- pre_hidden: bfloat16 [7680, 4096], P(('expert', 'shard')), may hold values from -12 to 12
- dec_resid: bfloat16 [16, 32, 4096], P('shard', 'expert'), may hold values from -12 to 12
- dec_query: bfloat16 [512, 4096], P('shard', 'expert'), may hold values from -4.5 to 4.5
- kv_pool: bfloat16 [8, 16896, 16, 256], P('expert', 'shard'), may hold values from -4.5 to 4.5
- page_table: int32 [16, 32, 128], P('shard'), may hold values from 0 to 1055, as said below
- cache_len: int32 [16, 32], P('shard'), may hold values from 2 to 2048, as said below
- out_weight: bfloat16 [4096, 4096], P('expert'), may hold values from -0.5 to 0.5
- norm_gain: float32 [4096], replicated, may hold values from 0.5 to 1.5
- route_ids_pre: int32 [7680, 2], P(('expert', 'shard')), may hold values from 0 to 7, as said below
- route_ids_dec: int32 [16, 32, 2], P('shard', 'expert'), may hold values from 0 to 7, as said below
- route_logit_pre: float32 [7680, 2], P(('expert', 'shard')), may hold values from -6 to 6
- route_logit_dec: float32 [16, 32, 2], P('shard', 'expert'), may hold values from -6 to 6
- expert_slot: int32 [8], replicated, may hold values from 0 to 7, each once
- w_gate: bfloat16 [8, 4096, 8192], P('expert', None, 'shard'), may hold values from -0.09375 to 0.09375
- w_up: bfloat16 [8, 4096, 8192], P('expert', None, 'shard'), may hold values from -0.09375 to 0.09375
- w_down: bfloat16 [8, 8192, 4096], P('expert', 'shard'), may hold values from -0.0625 to 0.0625
Outputs:
- mixed_pre: bfloat16 [7680, 4096], P(('expert', 'shard'))
- mixed_dec: bfloat16 [16, 32, 4096], P('shard', 'expert')
Inputs may be any that keep to these rules, and one draw needn't show every extreme that they name: `cache_len`: the requests of one shard index hold at most 16384 cached positions together, and one of them holds exactly 2048. `page_table`: for request i of shard index s, entries j below ceil(cache_len[s, i] / 16) name pages of the pool of that shard index, all distinct over the shard index; the other entries are unused. `route_ids_pre`: each row names two different experts. The rows of one device (its 60 prefill rows and its 4 decode rows) name each expert at most 18 times, and some expert exactly 18 times on every device. `route_ids_dec`: as for route_ids_pre: a device's decode rows count with its prefill rows.
All inputs are finite; a program needn't handle non-finite values.
Results may differ from a plain program's by a relative error of at most 0.015.
Values may be sent and summed in bfloat16 or wider, within the bound.
A program may use at most 192 MiB of HBM per device.

v0:
```python
import jax
import jax.numpy as jnp
from jax import lax
from jax.sharding import PartitionSpec as P


def table_attention(dec_query, kv_pool, page_rows, lengths):
    dec_dev, local_cols = dec_query.shape
    kv_local, pool_dev, page_size, twice_dim = kv_pool.shape
    head_dim = twice_dim // 2
    group_size = local_cols // (head_dim * kv_local)
    span_tokens = page_rows.shape[1] * page_size
    queries = dec_query.reshape(dec_dev, kv_local, group_size, head_dim)
    gathered = kv_pool[:, page_rows].reshape(kv_local, dec_dev, span_tokens, twice_dim)
    scores = jnp.einsum(
        "rkgd,krtd->rkgt", queries, gathered[..., :head_dim], preferred_element_type=jnp.float32
    ) * head_dim ** (-0.5)
    live_pos = (jnp.arange(span_tokens, dtype=jnp.int32)[None, :] < lengths[:, None])[
        :, None, None, :
    ]
    row_top = jnp.max(jnp.where(live_pos, scores, -jnp.inf), axis=-1, keepdims=True)
    weights_f = jnp.where(live_pos, jnp.exp(scores - row_top), 0.0)
    totals = jnp.sum(weights_f, axis=-1)
    weights_b = weights_f.astype(jnp.bfloat16)
    summed = jnp.einsum(
        "rkgt,krtd->rkgd", weights_b, gathered[..., head_dim:], preferred_element_type=jnp.float32
    )
    return (summed / totals[..., None]).astype(jnp.bfloat16).reshape(dec_dev, local_cols)


def local(
    pre_hidden,
    dec_resid,
    dec_query,
    kv_pool,
    page_table,
    cache_len,
    out_weight,
    norm_gain,
    route_ids_pre,
    route_ids_dec,
    route_logit_pre,
    route_logit_dec,
    expert_slot,
    w_gate,
    w_up,
    w_down,
):
    n_expert = lax.axis_size("expert")
    page_rows = page_table[0]
    lengths = cache_len[0]
    attn = table_attention(dec_query, kv_pool, page_rows, lengths)
    head_total = lax.psum_scatter(
        jnp.dot(attn, out_weight, preferred_element_type=jnp.float32).astype(jnp.bfloat16),
        "expert",
        scatter_dimension=0,
        tiled=True,
    ).astype(jnp.float32)
    h_dec = (dec_resid[0].astype(jnp.float32) + head_total).astype(jnp.bfloat16)
    hidden = jnp.concatenate([pre_hidden, h_dec], axis=0)
    route_ids = jnp.concatenate([route_ids_pre, route_ids_dec[0]], axis=0)
    logits = jnp.concatenate([route_logit_pre, route_logit_dec[0]], axis=0)
    pre_count = pre_hidden.shape[0]
    rows_dev, width = hidden.shape
    slot_cap = (rows_dev + 3) // 4 + 2
    stream = hidden.astype(jnp.float32)
    normed = (
        stream * lax.rsqrt(jnp.mean(stream * stream, axis=-1, keepdims=True) + 1e-05) * norm_gain
    ).astype(jnp.bfloat16)
    shares = jnp.stack(
        [jax.nn.sigmoid(logits[:, 0] - logits[:, 1]), jax.nn.sigmoid(logits[:, 1] - logits[:, 0])],
        axis=-1,
    )
    experts = expert_slot.shape[0]
    per_group = w_gate.shape[0]
    expert_ids = jnp.arange(experts, dtype=jnp.int32)
    slot_match = expert_slot[None, :] == expert_ids[:, None]
    slot_of = jnp.sum(jnp.where(slot_match, expert_ids[None, :], 0), axis=1)
    slot_ids = jnp.sum(jnp.where(route_ids[..., None] == expert_ids, slot_of, 0), axis=-1)
    flat_slots = slot_ids.reshape(-1)
    slot_hot = (flat_slots[:, None] == expert_ids[None, :]).astype(jnp.int32)
    ranking = jnp.sum((jnp.cumsum(slot_hot, axis=0) - slot_hot) * slot_hot, axis=1)
    slot_pos = (flat_slots * slot_cap + ranking).reshape(rows_dev, 2)
    slots_all = experts * slot_cap
    placing = jnp.any(
        jnp.arange(slots_all, dtype=jnp.int32)[:, None, None] == slot_pos[None], axis=-1
    ).astype(jnp.bfloat16)
    buffer = jnp.dot(placing, normed, preferred_element_type=jnp.float32).astype(jnp.bfloat16)
    buffer = buffer.reshape(n_expert, per_group, slot_cap, width)
    received = lax.all_to_all(buffer, "expert", split_axis=0, concat_axis=0, tiled=True)
    piece_rows = lax.all_gather(received[None], "shard", axis=0, tiled=True)
    gate = jnp.einsum("sgkcd,kdf->sgkcf", piece_rows, w_gate, preferred_element_type=jnp.float32)
    upper = jnp.einsum("sgkcd,kdf->sgkcf", piece_rows, w_up, preferred_element_type=jnp.float32)
    act = (jax.nn.silu(gate) * upper).astype(jnp.bfloat16)
    term = jnp.einsum("sgkcf,kfd->sgkcd", act, w_down, preferred_element_type=jnp.float32)
    own_rows = lax.psum_scatter(
        term.astype(jnp.bfloat16).astype(jnp.float32).astype(jnp.bfloat16),
        "shard",
        scatter_dimension=0,
        tiled=True,
    ).astype(jnp.float32)
    outputs = own_rows[0].astype(jnp.bfloat16)
    returned = lax.all_to_all(outputs, "expert", split_axis=0, concat_axis=0, tiled=True).reshape(
        slots_all, width
    )
    picked = returned[slot_pos]
    mixed_rows = stream + jnp.sum(shares[..., None] * picked.astype(jnp.float32), axis=1)
    mixed_out = mixed_rows.astype(jnp.bfloat16)
    return (mixed_out[:pre_count], mixed_out[pre_count:][None])


def solution(mesh):
    placed = (
        P(("expert", "shard"), None),
        P("shard", "expert", None),
        P("shard", "expert"),
        P("expert", "shard", None, None),
        P("shard", None, None),
        P("shard", None),
        P("expert", None),
        P(),
        P(("expert", "shard"), None),
        P("shard", "expert", None),
        P(("expert", "shard"), None),
        P("shard", "expert", None),
        P(),
        P("expert", None, "shard"),
        P("expert", None, "shard"),
        P("expert", "shard", None),
    )
    return jax.shard_map(
        local,
        mesh=mesh,
        in_specs=placed,
        out_specs=(P(("expert", "shard"), None), P("shard", "expert", None)),
        check_vma=False,
    )
```

profile of v0, /device:TPU:0, one launch (start us, length us, event | category | flops | bytes accessed | tf_op | source)
XLA Modules:
  0.0 599.9 jit_solution(9120764802494427658)
XLA Ops:
  7.2 0.7 fusion.44
  7.9 0.8 reshape.189
  8.7 0.8 iota_compare_fusion
  9.5 40.6 %gather_fusion = bf16[4096,16,256]{2,1,0:T(8,128)(2,1)} fusion(bf16[1056,16,256]{2,1,0:T(8,128)(2,1)} %bitcast.140, s32[4096]{0:T(1024)S(1)} %fusion.44), kind=kCustom, calls=%fused_computation | custom fusion | bytes 67125248 | tf_op jit(solution)/shard_map/gather | solution.py:14
  50.1 8.0 %fusion.24 = f32[32,2048,4]{1,2,0:T(4,128)S(1)} fusion(bf16[32,4,128]{2,1,0:T(4,128)(2,1)S(1)} %reshape.189, bf16[1,32,2048,256]{3,2,1,0:T(8,128)(2,1)} %bitcast.141), kind=kOutput, calls=%fused_computation.28 | convolution fusion | flops 67371008 | bytes 17858560 | tf_op jit(solution)/shard_map/rkgd,krtd->rkgt/dot_general | solution.py:15
  58.1 1.1 fusion.48
  59.3 7.2 %fusion.27 = bf16[32,4,128]{2,1,0:T(4,128)(2,1)S(1)} fusion(bf16[1,32,2048,256]{3,2,1,0:T(8,128)(2,1)} %bitcast.142, bf16[32,4,2048]{2,1,0:T(4,128)(2,1)S(1)} %get-tuple-element.5, f32[32,4]{1,0:T(8,128)S(1)} %get-tuple-element.4), kind=kOutput, calls=%fused_computation.36 | convolution fusion | flops 67141632 | bytes 17334784 | tf_op jit(solution)/shard_map/rkgt,krtd->rkgd/dot_general | solution.py:25
  66.5 1.5 convolution_convert_fusion.1
  68.8 0.2 reduce_window_sum.11
  69.3 0.6 dynamic-slice
  70.7 73.8 %all-reduce.3.cloned.1.call-done = bf16[32,4096]{1,0:T(8,128)(2,1)} async-done(((bf16[32,4096]{1,0:T(8,128)(2,1)}), bf16[32,4096]{1,0:T(8,128)(2,1)}) %all-reduce.3.cloned.1.call-update) | async-done | bytes 262160
  144.5 0.9 fusion.39
  145.4 0.2 fusion.28
  145.6 0.5 convolution_convert_fusion
  146.1 0.4 reshape.192
  146.6 18.4 %all_to_all.10 = bf16[8,1,18,4096]{3,2,1,0:T(8,128)(2,1)S(1)} all-to-all(bf16[8,1,18,4096]{3,2,1,0:T(8,128)(2,1)S(1)} %bitcast.145), channel_id=1, replica_groups=mesh['expert'=8,'shard'=16] {'expert'}, dimensions={0} | all-to-all | bytes 2359296 | tf_op jit(solution)/shard_map/all_to_all | solution.py:90
  165.0 1.7 copy.41
  166.7 0.2 reduce-scatter.2.cloned.1.call-start
  166.9 119.6 %all-gather.3.cloned.1.call-done = bf16[128,1,18,4096]{3,0,2,1:T(8,128)(2,1)} async-done(((bf16[8,1,18,4096]{3,0,2,1:T(8,128)(2,1)}), bf16[128,1,18,4096]{3,0,2,1:T(8,128)(2,1)}) %all-gather.3.cloned.1.call-update) | async-done | bytes 18874384 | tf_op jit(solution)/shard_map/all_gather | solution.py:91
  286.6 16.0 %copy.42 = bf16[128,1,18,4096]{3,2,0,1:T(8,128)(2,1)S(1)} copy(bf16[128,1,18,4096]{3,0,2,1:T(8,128)(2,1)} %all-gather.3.cloned.1.call-done) | data formatting | bytes 37748736 | tf_op jit(solution)/shard_map/all_gather | solution.py:91
  302.6 8.3 %copy-done = bf16[128,1,18,4096]{3,2,0,1:T(8,128)(2,1)} copy-done((bf16[128,1,18,4096]{3,2,0,1:T(8,128)(2,1)}, bf16[128,1,18,4096]{3,2,0,1:T(8,128)(2,1)S(1)}, u32[]{:S(2)}) %copy-start) | copy-done | bytes 18874392
  310.9 17.8 %fusion.12 = f32[16,8,18,512]{3,2,1,0:T(8,128)} fusion(bf16[16,8,18,4096]{3,2,1,0:T(8,128)(2,1)S(1)} %bitcast.143, bf16[1,4096,512]{2,1,0:T(8,128)(2,1)} %param.29), kind=kOutput, calls=%fused_computation.20 | convolution fusion | flops 9663676416 | bytes 27787264 | tf_op jit(solution)/shard_map/sgkcd,kdf->sgkcf/dot_general | solution.py:92
  328.7 19.8 %fusion.64 = bf16[16,8,18,512]{3,2,1,0:T(8,128)(2,1)} fusion(bf16[16,8,18,4096]{3,2,1,0:T(8,128)(2,1)} %bitcast.144, bf16[1,4096,512]{2,1,0:T(8,128)(2,1)} %param.30, f32[16,8,18,512]{3,2,1,0:T(8,128)} %fusion.12), kind=kOutput, calls=%fused_computation.22.clone.1 | convolution fusion | flops 9670754304 | bytes 30146560 | tf_op jit(solution)/shard_map/sgkcd,kdf->sgkcf/dot_general | solution.py:93
  348.4 20.6 %convert_bitcast_fusion = bf16[16,8,1,18,4096]{4,3,1,0,2:T(8,128)(2,1)} fusion(bf16[1,512,4096]{2,1,0:T(8,128)(2,1)} %param.31, bf16[16,8,18,512]{3,2,1,0:T(8,128)(2,1)} %fusion.64), kind=kOutput, calls=%fused_computation.3 | convolution fusion | flops 9673113600 | bytes 25427968 | tf_op jit(solution)/shard_map/sgkcf,kfd->sgkcd/dot_general | solution.py:95
  369.0 188.4 %reduce-scatter.2.cloned.1.call-done = bf16[1,8,1,18,4096]{4,3,1,0,2:T(8,128)(2,1)} async-done(((bf16[16,8,1,18,4096]{4,3,1,0,2:T(8,128)(2,1)}), bf16[1,8,1,18,4096]{4,3,1,0,2:T(8,128)(2,1)}) %reduce-scatter.2.cloned.1.call-update) | async-done | bytes 1179664 | tf_op jit(solution)/shard_map/reduce_scatter | solution.py:96
  557.4 4.4 all-to-all-start.1
  562.5 21.8 %all-to-all-done.1 = bf16[8,1,18,4096]{3,2,1,0:T(8,128)(2,1)S(1)} async-done(((bf16[8,1,18,4096]{3,2,1,0:T(8,128)(2,1)}), bf16[8,1,18,4096]{3,2,1,0:T(8,128)(2,1)S(1)}, u32[]{:S(2)}, u32[]{:S(2)}) %all-to-all-start.1) | async-done | bytes 1179680 | tf_op jit(solution)/shard_map/all_to_all | solution.py:103
  584.3 0.4 reshape.198
  584.7 2.2 gather_fusion.1
  586.9 2.4 reshape.224
  589.3 3.1 multiply_reduce_fusion
  592.6 0.7 slice_bitcast_fusion.10
  (51 shorter events, 2.2 us)
Async XLA Ops:
  7.2 137.3 %all-reduce.3.cloned.1.call-start = ((), (), s32[]{:S(2)}) async-start(), calls=%async_computation.5 | async-start | bytes 524288
  59.2 7.3 %copy-start.2 = (bf16[512,4096]{1,0:T(8,128)(2,1)S(1)}, bf16[512,4096]{1,0:T(8,128)(2,1)}, u32[]{:S(2)}) copy-start(bf16[512,4096]{1,0:T(8,128)(2,1)} %param.22) | copy-start | bytes 12582916
  59.2 8.9 %copy-start.10 = (s32[8]{0:T(128)S(1)}, s32[8]{0:T(128)}, u32[]{:S(2)}) copy-start(s32[8]{0:T(128)} %param.28) | copy-start | bytes 100
  59.2 9.0 %copy-start.6 = (s32[1,4,2]{1,2,0:T(2,128)S(1)}, s32[1,4,2]{1,2,0:T(2,128)}, u32[]{:S(2)}) copy-start(s32[1,4,2]{1,2,0:T(2,128)} %param.25) | copy-start | bytes 100
  59.2 9.0 %copy-start.7 = (s32[60,2]{0,1:T(2,128)S(1)}, s32[60,2]{0,1:T(2,128)}, u32[]{:S(2)}) copy-start(s32[60,2]{0,1:T(2,128)} %param.24) | copy-start | bytes 1444
  59.2 10.1 %copy-start.11 = (u32[128]{0:T(128)S(1)}, u32[128]{0:T(128)}, u32[]{:S(2)}) copy-start(u32[128]{0:T(128)} %constant.45) | copy-start | bytes 1540
  59.3 85.2 %copy-start.4 = (bf16[1,4,4096]{2,1,0:T(4,128)(2,1)S(1)}, bf16[1,4,4096]{2,1,0:T(4,128)(2,1)}, u32[]{:S(2)}) copy-start(bf16[1,4,4096]{2,1,0:T(4,128)(2,1)} %param.17) | copy-start | bytes 98308
  59.3 86.1 %copy-start.1 = (bf16[60,4096]{1,0:T(8,128)(2,1)S(1)}, bf16[60,4096]{1,0:T(8,128)(2,1)}, u32[]{:S(2)}) copy-start(bf16[60,4096]{1,0:T(8,128)(2,1)} %param.16) | copy-start | bytes 1474564
  59.3 86.3 %copy-start.5 = (f32[4096]{0:T(1024)S(1)}, f32[4096]{0:T(1024)}, u32[]{:S(2)}) copy-start(f32[4096]{0:T(1024)} %param.23) | copy-start | bytes 49156
  68.1 218.5 %all-gather.3.cloned.1.call-start = ((), (), s32[]{:S(2)}) async-start(), calls=%async_computation.4 | async-start | bytes 20054016 | tf_op jit(solution)/shard_map/all_gather | solution.py:91
  166.7 390.7 %reduce-scatter.2.cloned.1.call-start = ((), (), s32[]{:S(2)}) async-start(), calls=%async_computation.3 | async-start | bytes 26738688 | tf_op jit(solution)/shard_map/reduce_scatter | solution.py:96
  302.6 8.3 %copy-start = (bf16[128,1,18,4096]{3,2,0,1:T(8,128)(2,1)}, bf16[128,1,18,4096]{3,2,0,1:T(8,128)(2,1)S(1)}, u32[]{:S(2)}) copy-start(bf16[128,1,18,4096]{3,2,0,1:T(8,128)(2,1)S(1)} %copy.42) | copy-start | bytes 56623108
  369.0 193.3 %copy-start.8 = (f32[1,4,2]{1,2,0:T(2,128)S(1)}, f32[1,4,2]{1,2,0:T(2,128)}, u32[]{:S(2)}) copy-start(f32[1,4,2]{1,2,0:T(2,128)} %param.27) | copy-start | bytes 100
  369.0 193.3 %copy-start.9 = (f32[60,2]{0,1:T(2,128)S(1)}, f32[60,2]{0,1:T(2,128)}, u32[]{:S(2)}) copy-start(f32[60,2]{0,1:T(2,128)} %param.26) | copy-start | bytes 1444
  557.4 26.9 %all-to-all-start.1 = ((bf16[8,1,18,4096]{3,2,1,0:T(8,128)(2,1)}), bf16[8,1,18,4096]{3,2,1,0:T(8,128)(2,1)S(1)}, u32[]{:S(2)}, u32[]{:S(2)}) async-start(bf16[8,1,18,4096]{3,2,1,0:T(8,128)(2,1)} %bitcast.146), calls=%async_computation.2 | async-start | bytes 3145728 | tf_op jit(solution)/shard_map/all_to_all | solution.py:103
  592.6 0.8 copy-start.3
Sparse Core Ops, SparseCore 0:
  68.2 76.2 all-reduce.2
  166.8 119.6 all-gather.2
  369.2 188.1 reduce-scatter.1
where the time goes:
time: 601 us; the launch traced here: 600 us
  waiting for transfers between devices  404 us (67%)
  matrix products  75.5 us (13%)
  local copies, waits for them, and re-layouts  75.2 us (13%)
  blocking collectives  18.4 us (3%)
  between operations  14.7 us (2%)
  other arithmetic  7.84 us (1%)
    reduce_scatter x1, waiting for transfers between devices, local(): lax.psum_scatter(term.astype(jnp.bfloat16).astype(jnp.float32).astype(jnp...  188 us
    all_gather x1, waiting for transfers between devices, local(): piece_rows = lax.all_gather(received[None], 'shard', axis=0, tiled=True)  120 us
    unnamed x4, waiting for transfers between devices  73.8 us
    gather x1, local copies, waits for them, and re-layouts, table_attention(): kv_pool[:, page_rows].reshape(kv_local, dec_dev, span_tokens, twice_dim)  40.6 us
    all_to_all x1, waiting for transfers between devices, local(): lax.all_to_all(outputs, 'expert', split_axis=0, concat_axis=0, tiled=True)  21.8 us
    dot_general x1, matrix products, local(): jnp.einsum('sgkcf,kfd->sgkcd', act, w_down, preferred_element_type=jnp.fl...  20.6 us
    dot_general x1, matrix products, local(): jnp.einsum('sgkcd,kdf->sgkcf', piece_rows, w_up, preferred_element_type=j...  19.8 us
    all_to_all x1, blocking collectives, local(): lax.all_to_all(buffer, 'expert', split_axis=0, concat_axis=0, tiled=True)  18.4 us
  transfers between devices with their start and end apart: 4, of which 4 were waited for; matrix products, arithmetic and copies ran while one was open for 0% of the time, Pallas kernels for 0%

commit v1 on v0

v1 whole, which is shorter than its diff:
```python
import jax
import jax.numpy as jnp
from jax import lax
from jax.experimental import pallas as pl
from jax.experimental.pallas import tpu as pltpu
from jax.sharding import PartitionSpec as P

MESH = pl.DeviceIdType.MESH
X_CHIPS = 4
CORES = 2
Z_HALVES = 2
SHARD_PLANE = X_CHIPS * CORES
LOWEST = -1e30


def attention_kernel(q_ref, count_ref, kv_ref, out_ref, top, total, summed):
    step = pl.program_id(0)

    @pl.when(step == 0)
    def _():
        top[...] = jnp.full(top.shape, LOWEST, jnp.float32)
        total[...] = jnp.zeros(total.shape, jnp.float32)
        summed[...] = jnp.zeros(summed.shape, jnp.float32)

    head_dim = q_ref.shape[1]
    positions = kv_ref.shape[0]
    pages = count_ref.shape[2]
    page_size = positions // pages
    scores = lax.dot_general(
        q_ref[...], kv_ref[:, :head_dim], (((1,), (1,)), ((), ())), preferred_element_type=jnp.float32
    ) * head_dim ** (-0.5)
    page_of = lax.broadcasted_iota(jnp.int32, (pages, positions), 1) // page_size
    spread = (page_of == lax.broadcasted_iota(jnp.int32, (pages, positions), 0)).astype(jnp.bfloat16)
    counts = jnp.dot(count_ref[0], spread, preferred_element_type=jnp.float32)
    offset = (lax.broadcasted_iota(jnp.int32, (1, positions), 1) % page_size).astype(jnp.float32)
    live = counts > offset
    scores = jnp.where(live, scores, LOWEST)
    new_top = jnp.maximum(top[...], jnp.max(scores, axis=1, keepdims=True))
    scale = jnp.exp(top[...] - new_top)
    weights = jnp.where(live, jnp.exp(scores - new_top), 0.0)
    top[...] = new_top
    total[...] = total[...] * scale + jnp.sum(weights, axis=1, keepdims=True)
    summed[...] = summed[...] * scale + jnp.dot(
        weights.astype(jnp.bfloat16), kv_ref[:, head_dim:], preferred_element_type=jnp.float32
    )

    @pl.when(step == pl.num_programs(0) - 1)
    def _():
        out_ref[...] = (summed[...] / total[...]).astype(out_ref.dtype)


def pool_attention(dec_query, kv_pool, page_rows, lengths):
    dec_dev, local_cols = dec_query.shape
    _, pool_dev, page_size, twice_dim = kv_pool.shape
    head_dim = twice_dim // 2
    group = local_cols // head_dim
    max_pages = page_rows.shape[1]
    steps = 16
    pages = pool_dev // steps
    in_page = jnp.clip(
        lengths[:, None] - page_size * jnp.arange(max_pages, dtype=jnp.int32)[None, :], 0, page_size
    )
    pool_ids = jnp.arange(pool_dev, dtype=jnp.int32)
    counts = jnp.sum(
        jnp.where(page_rows[:, :, None] == pool_ids[None, None, :], in_page[:, :, None], 0), axis=1
    ).astype(jnp.bfloat16)
    counts = jnp.repeat(counts, group, axis=0).reshape(dec_dev * group, steps, pages).transpose(1, 0, 2)
    rows = dec_dev * group
    return pl.pallas_call(
        attention_kernel,
        grid=(steps,),
        in_specs=[
            pl.BlockSpec((rows, head_dim), lambda i: (0, 0)),
            pl.BlockSpec((1, rows, pages), lambda i: (i, 0, 0)),
            pl.BlockSpec((pages * page_size, twice_dim), lambda i: (i, 0)),
        ],
        out_specs=pl.BlockSpec((rows, head_dim), lambda i: (0, 0)),
        out_shape=jax.ShapeDtypeStruct((rows, head_dim), jnp.bfloat16),
        scratch_shapes=[
            pltpu.VMEM((rows, 1), jnp.float32),
            pltpu.VMEM((rows, 1), jnp.float32),
            pltpu.VMEM((rows, head_dim), jnp.float32),
        ],
        cost_estimate=pl.CostEstimate(
            flops=4 * rows * head_dim * pool_dev * page_size,
            bytes_accessed=pool_dev * page_size * twice_dim * 2,
            transcendentals=rows * pool_dev * page_size,
        ),
        name="pool_attention",
    )(dec_query.reshape(rows, head_dim), counts, kv_pool.reshape(pool_dev * page_size, twice_dim)).reshape(
        dec_dev, local_cols
    )


def plane_kernel(per_half, n_expert, src_ref, dst_ref, send_sem, recv_sem, own_sem):
    expert = lax.axis_index("expert")
    shard = lax.axis_index("shard")
    half, rest = shard // SHARD_PLANE, shard % SHARD_PLANE
    mine = half * n_expert + expert

    def peer(step):
        to_expert = (expert + step % n_expert) % n_expert
        to_half = (half + step // n_expert) % Z_HALVES
        return to_expert, to_half

    peers = Z_HALVES * n_expert
    barrier = pltpu.get_barrier_semaphore()
    for step in range(1, peers):
        to_expert, to_half = peer(step)
        pl.semaphore_signal(
            barrier, inc=1, device_id=(to_expert, to_half * SHARD_PLANE + rest), device_id_type=MESH
        )
    pl.semaphore_wait(barrier, peers - 1)
    copies = []
    for step in range(1, peers):
        to_expert, to_half = peer(step)
        block = to_half * n_expert + to_expert if per_half else to_expert
        copy = pltpu.make_async_remote_copy(
            src_ref=src_ref.at[block],
            dst_ref=dst_ref.at[mine],
            send_sem=send_sem.at[step],
            recv_sem=recv_sem.at[step],
            device_id=(to_expert, to_half * SHARD_PLANE + rest),
            device_id_type=MESH,
        )
        copy.start()
        copies.append(copy)
    own = pltpu.make_async_copy(src_ref.at[mine if per_half else expert], dst_ref.at[mine], own_sem)
    own.start()
    own.wait()
    for copy in copies:
        copy.wait()


def plane_exchange(blocks, n_expert, per_half, collective_id):
    peers = Z_HALVES * n_expert
    block = blocks.shape[1:]

    def kernel(*refs):
        plane_kernel(per_half, n_expert, *refs)

    return pl.pallas_call(
        kernel,
        out_shape=jax.ShapeDtypeStruct((peers,) + block, blocks.dtype),
        in_specs=[pl.BlockSpec(memory_space=pl.ANY)],
        out_specs=pl.BlockSpec(memory_space=pl.ANY),
        scratch_shapes=[
            pltpu.SemaphoreType.DMA((peers,)),
            pltpu.SemaphoreType.DMA((peers,)),
            pltpu.SemaphoreType.DMA,
        ],
        compiler_params=pltpu.CompilerParams(collective_id=collective_id, has_side_effects=True),
        name="plane_return" if per_half else "plane_send",
    )(blocks)


def expert_kernel(
    rows_ref, gate0, gate1, up0, up1, down0, down1, out_ref,
    held, partial, direct, relayed, act, gate, up, down,
    send_sem, recv_sem, load_sem,
):
    expert = lax.axis_index("expert")
    shard = lax.axis_index("shard")
    half, rest = shard // SHARD_PLANE, shard % SHARD_PLANE
    chip, core = rest // CORES, rest % CORES
    right = half * SHARD_PLANE + (chip + 1) % X_CHIPS * CORES + core
    left = half * SHARD_PLANE + (chip + X_CHIPS - 1) % X_CHIPS * CORES + core
    count = rows_ref.shape[0]
    part = count // 2
    low, high = pl.ds(0, part), pl.ds(part, part)

    loads = []
    for at, (src, dst) in enumerate(
        ((gate0, gate.at[0]), (up0, up.at[0]), (gate1, gate.at[1]), (up1, up.at[1]), (down0, down.at[0]), (down1, down.at[1]))
    ):
        load = pltpu.make_async_copy(src, dst, load_sem.at[at])
        load.start()
        loads.append(load)

    barrier = pltpu.get_barrier_semaphore()
    for neighbour in (left, right):
        pl.semaphore_signal(barrier, inc=1, device_id=(expert, neighbour), device_id_type=MESH)
    pl.semaphore_wait(barrier, 2)

    def send(at, src, dst, to):
        copy = pltpu.make_async_remote_copy(
            src_ref=src,
            dst_ref=dst,
            send_sem=send_sem.at[at],
            recv_sem=recv_sem.at[at],
            device_id=(expert, to),
            device_id_type=MESH,
        )
        copy.start()
        return copy

    first_r = send(0, rows_ref.at[low], held.at[0, low], right)
    first_l = send(1, rows_ref.at[high], held.at[0, high], left)
    second_r = send(2, rows_ref.at[high], held.at[1, high], right)
    second_l = send(3, rows_ref.at[low], held.at[1, low], left)
    for load in loads:
        load.wait()

    width = rows_ref.shape[1]
    ff = gate.shape[2]
    tile = 256
    wide = 512

    def feed_forward(src, dst):
        for side in range(2):
            @pl.loop(0, ff // tile)
            def _(t):
                columns = pl.ds(pl.multiple_of(t * tile, tile), tile)
                g = jnp.dot(src[...], gate[side, :, columns], preferred_element_type=jnp.float32)
                u = jnp.dot(src[...], up[side, :, columns], preferred_element_type=jnp.float32)
                act[side, :, columns] = (g / (1.0 + jnp.exp(-g)) * u).astype(act.dtype)

        @pl.loop(0, width // wide)
        def _(t):
            columns = pl.ds(pl.multiple_of(t * wide, wide), wide)
            o = jnp.dot(act[0], down[0, :, columns], preferred_element_type=jnp.float32)
            o = o + jnp.dot(act[1], down[1, :, columns], preferred_element_type=jnp.float32)
            dst[:, columns] = o.astype(dst.dtype)

    feed_forward(rows_ref, partial.at[3])
    first_r.wait_recv()
    third_r = send(4, held.at[0, low], held.at[2, low], right)
    first_l.wait_recv()
    third_l = send(5, held.at[0, high], held.at[2, high], left)
    feed_forward(held.at[0], partial.at[0])
    plain_r = send(6, partial.at[0, high], direct.at[0, high], right)
    plain_l = send(7, partial.at[0, low], direct.at[1, low], left)
    second_r.wait_recv()
    second_l.wait_recv()
    feed_forward(held.at[1], partial.at[1])
    third_r.wait_recv()
    third_l.wait_recv()
    feed_forward(held.at[2], partial.at[2])
    far_r = send(8, partial.at[2, low], relayed.at[low], right)
    far_l = send(9, partial.at[2, high], relayed.at[high], left)

    strip = 48

    def add_relayed(start):
        @pl.loop(0, part // strip)
        def _(t):
            lines = pl.ds(pl.multiple_of(start + t * strip, 16), strip)
            partial[1, lines, :] = (
                partial[1, lines, :].astype(jnp.float32) + relayed[lines, :].astype(jnp.float32)
            ).astype(partial.dtype)

    far_r.wait_recv()
    add_relayed(0)
    joined_r = send(10, partial.at[1, low], direct.at[0, low], right)
    far_l.wait_recv()
    add_relayed(part)
    joined_l = send(11, partial.at[1, high], direct.at[1, high], left)
    plain_r.wait_recv()
    plain_l.wait_recv()
    joined_r.wait_recv()
    joined_l.wait_recv()

    @pl.loop(0, count // strip)
    def _(t):
        lines = pl.ds(pl.multiple_of(t * strip, 16), strip)
        out_ref[lines, :] = (
            partial[3, lines, :].astype(jnp.float32)
            + direct[0, lines, :].astype(jnp.float32)
            + direct[1, lines, :].astype(jnp.float32)
        ).astype(out_ref.dtype)

    for copy in (
        first_r, first_l, second_r, second_l, third_r, third_l,
        plain_r, plain_l, far_r, far_l, joined_r, joined_l,
    ):
        copy.wait_send()


def expert_exchange(rows, gates, ups, downs, collective_id):
    count, width = rows.shape
    ff = gates[0].shape[1]
    bf16 = jnp.bfloat16
    vmem = pl.BlockSpec(memory_space=pltpu.VMEM)
    anywhere = pl.BlockSpec(memory_space=pl.ANY)
    return pl.pallas_call(
        expert_kernel,
        out_shape=jax.ShapeDtypeStruct((count, width), bf16),
        in_specs=[vmem] + [anywhere] * 6,
        out_specs=vmem,
        scratch_shapes=[
            pltpu.VMEM((3, count, width), bf16),
            pltpu.VMEM((4, count, width), bf16),
            pltpu.VMEM((2, count, width), bf16),
            pltpu.VMEM((count, width), bf16),
            pltpu.VMEM((2, count, ff), bf16),
            pltpu.VMEM((2, width, ff), bf16),
            pltpu.VMEM((2, width, ff), bf16),
            pltpu.VMEM((2, ff, width), bf16),
            pltpu.SemaphoreType.DMA((12,)),
            pltpu.SemaphoreType.DMA((12,)),
            pltpu.SemaphoreType.DMA((6,)),
        ],
        compiler_params=pltpu.CompilerParams(
            collective_id=collective_id, has_side_effects=True, vmem_limit_bytes=66 * 1024 * 1000 - 560000
        ),
        name="expert_exchange",
    )(rows, *gates, *ups, *downs)


def local(
    pre_hidden,
    dec_resid,
    dec_query,
    kv_pool,
    page_table,
    cache_len,
    out_weight,
    norm_gain,
    route_ids_pre,
    route_ids_dec,
    route_logit_pre,
    route_logit_dec,
    expert_slot,
    w_gate,
    w_up,
    w_down,
):
    n_expert = lax.axis_size("expert")
    n_shard = lax.axis_size("shard")
    swap = [(at, at ^ 1) for at in range(n_shard)]
    gates = (w_gate[0], lax.ppermute(w_gate[0], "shard", swap))
    ups = (w_up[0], lax.ppermute(w_up[0], "shard", swap))
    downs = (w_down[0], lax.ppermute(w_down[0], "shard", swap))
    attn = pool_attention(dec_query, kv_pool, page_table[0], cache_len[0])
    head_part = jnp.dot(attn, out_weight, preferred_element_type=jnp.float32).astype(jnp.bfloat16)
    head_parts = lax.all_to_all(
        head_part.reshape(n_expert, -1, head_part.shape[1]), "expert", split_axis=0, concat_axis=0, tiled=True
    )
    head_total = jnp.sum(head_parts.astype(jnp.float32), axis=0)
    h_dec = (dec_resid[0].astype(jnp.float32) + head_total).astype(jnp.bfloat16)
    hidden = jnp.concatenate([pre_hidden, h_dec], axis=0)
    route_ids = jnp.concatenate([route_ids_pre, route_ids_dec[0]], axis=0)
    logits = jnp.concatenate([route_logit_pre, route_logit_dec[0]], axis=0)
    pre_count = pre_hidden.shape[0]
    rows_dev, width = hidden.shape
    slot_cap = (rows_dev + 3) // 4 + 2
    stream = hidden.astype(jnp.float32)
    normed = (
        stream * lax.rsqrt(jnp.mean(stream * stream, axis=-1, keepdims=True) + 1e-05) * norm_gain
    ).astype(jnp.bfloat16)
    shares = jnp.stack(
        [jax.nn.sigmoid(logits[:, 0] - logits[:, 1]), jax.nn.sigmoid(logits[:, 1] - logits[:, 0])],
        axis=-1,
    )
    experts = expert_slot.shape[0]
    expert_ids = jnp.arange(experts, dtype=jnp.int32)
    slot_match = expert_slot[None, :] == expert_ids[:, None]
    slot_of = jnp.sum(jnp.where(slot_match, expert_ids[None, :], 0), axis=1)
    slot_ids = jnp.sum(jnp.where(route_ids[..., None] == expert_ids, slot_of, 0), axis=-1)
    flat_slots = slot_ids.reshape(-1)
    slot_hot = (flat_slots[:, None] == expert_ids[None, :]).astype(jnp.int32)
    ranking = jnp.sum((jnp.cumsum(slot_hot, axis=0) - slot_hot) * slot_hot, axis=1)
    slot_pos = (flat_slots * slot_cap + ranking).reshape(rows_dev, 2)
    slots_all = experts * slot_cap
    chosen = jnp.arange(slots_all, dtype=jnp.int32)[:, None, None] == slot_pos[None]
    placing = jnp.any(chosen, axis=-1).astype(jnp.bfloat16)
    buffer = jnp.dot(placing, normed, preferred_element_type=jnp.float32).astype(jnp.bfloat16)
    lanes = 128
    buffer = buffer.reshape(experts, slot_cap, width // lanes, lanes)
    received = plane_exchange(buffer, n_expert, False, 0)
    rows = received.reshape(-1, width)
    sums = expert_exchange(rows, gates, ups, downs, 1)
    returned = plane_exchange(
        sums.reshape(Z_HALVES * n_expert, slot_cap, width // lanes, lanes), n_expert, True, 2
    ).reshape(Z_HALVES, slots_all, width)
    outputs = (returned[0].astype(jnp.float32) + returned[1].astype(jnp.float32)).astype(jnp.bfloat16)
    picking = (slot_pos.T.reshape(-1)[:, None] == jnp.arange(slots_all, dtype=jnp.int32)[None, :]).astype(
        jnp.bfloat16
    )
    picked = jnp.dot(picking, outputs, preferred_element_type=jnp.float32).reshape(2, rows_dev, width)
    mixed_rows = stream + shares[:, :1] * picked[0] + shares[:, 1:] * picked[1]
    mixed_out = mixed_rows.astype(jnp.bfloat16)
    return (mixed_out[:pre_count], mixed_out[pre_count:][None])


def solution(mesh):
    placed = (
        P(("expert", "shard"), None),
        P("shard", "expert", None),
        P("shard", "expert"),
        P("expert", "shard", None, None),
        P("shard", None, None),
        P("shard", None),
        P("expert", None),
        P(),
        P(("expert", "shard"), None),
        P("shard", "expert", None),
        P(("expert", "shard"), None),
        P("shard", "expert", None),
        P(),
        P("expert", None, "shard"),
        P("expert", None, "shard"),
        P("expert", "shard", None),
    )
    return jax.shard_map(
        local,
        mesh=mesh,
        in_specs=placed,
        out_specs=(P(("expert", "shard"), None), P("shard", "expert", None)),
        check_vma=False,
    )
```

time: 601 us -> 299 us (0.50)
  waiting for transfers between devices: 404 us -> 6.01 us
  Pallas kernels: 0 us -> 253 us
  matrix products: 75.5 us -> 4.18 us
  local copies, waits for them, and re-layouts: 75.2 us -> 15.6 us
  blocking collectives: 18.4 us -> 0 us
  between operations: 14.7 us -> 0.91 us
    pallas_call x0 -> x4, Pallas kernels: none -> 253 us  [the longest x1 158 us: expert_exchange(): pl.pallas_call(expert_kernel, out_shape=jax.ShapeDtypeStruct((count, widt...]
    reduce_scatter x1 -> x0, waiting for transfers between devices: 188 us -> none  [local(): lax.psum_scatter(term.astype(jnp.bfloat16).astype(jnp.float32).astype(jnp...]
    all_gather x1 -> x0, waiting for transfers between devices: 120 us -> none  [local(): piece_rows = lax.all_gather(received[None], 'shard', axis=0, tiled=True)]
    unnamed x4 -> x0, waiting for transfers between devices: 73.8 us -> none
    dot_general x5 -> x1, matrix products: 73.4 us -> 0.57 us  [local(): jnp.dot(picking, outputs, preferred_element_type=jnp.float32)]
    gather x2 -> x0, local copies, waits for them, and re-layouts: 42.8 us -> none  [the longest x1 40.6 us: table_attention(): kv_pool[:, page_rows].reshape(kv_local, dec_dev, span_tokens, twice_dim)]
    all_to_all x1 -> x0, blocking collectives: 18.4 us -> none  [local(): lax.all_to_all(buffer, 'expert', split_axis=0, concat_axis=0, tiled=True)]
    all_gather x1 -> x0, local copies, waits for them, and re-layouts: 16 us -> none  [local(): piece_rows = lax.all_gather(received[None], 'shard', axis=0, tiled=True)]
  transfers between devices with their start and end apart: 4 -> 4, of which waited for: 4 -> 1; matrix products, arithmetic and copies ran while one was open for 0% -> 7% of each run, Pallas kernels for 0% -> 19%
where the time goes in v1:
time: 299 us; the launch traced here: 296 us
  Pallas kernels  253 us (85%)
  local copies, waits for them, and re-layouts  15.6 us (5%)
  other arithmetic  9.89 us (3%)
  starting transfers between devices  6.59 us (2%)
  waiting for transfers between devices  6.01 us (2%)
  matrix products  4.18 us (1%)
    pallas_call x1, Pallas kernels, expert_exchange(): pl.pallas_call(expert_kernel, out_shape=jax.ShapeDtypeStruct((count, widt...  158 us
    pallas_call x2, Pallas kernels, plane_exchange(): pl.pallas_call(kernel, out_shape=jax.ShapeDtypeStruct((peers,) + block, b...  78.1 us
    pallas_call x1, Pallas kernels, pool_attention(): pl.pallas_call(attention_kernel, grid=(steps,), in_specs=[pl.BlockSpec((r...  16.9 us
    unnamed x29, local copies, waits for them, and re-layouts  10.1 us
    all_to_all x1, waiting for transfers between devices, local(): lax.all_to_all(head_part.reshape(n_expert, -1, head_part.shape[1]), 'expe...  6 us
  transfers between devices with their start and end apart: 4, of which 1 were waited for; matrix products, arithmetic and copies ran while one was open for 7% of the time, Pallas kernels for 19%

profile of v1, /device:TPU:0, one launch (start us, length us, event | category | flops | bytes accessed | tf_op | source)
XLA Modules:
  0.0 296.4 jit_solution(7193860461363173702)
XLA Ops:
  0.7 0.5 collective-permute-start.1
  1.3 0.7 subtract_clamp_fusion
  2.1 5.7 %select_reduce_fusion = s32[32,1056]{1,0:T(8,128)S(1)} fusion(s32[32,128]{1,0:T(8,128)S(1)} %subtract_clamp_fusion, s32[32,128]{1,0:T(8,128)} %bitcast.57), kind=kLoop, calls=%fused_computation | loop fusion | flops 12942336 | bytes 167936 | tf_op jit(solution)/shard_map/reduce_sum | solution.py:64
  7.8 0.9 reshape_reshape.3
  8.8 0.9 copy.37
  9.7 0.6 reshape.103.q_ref
  10.4 16.9 %pool_attention.1 = bf16[128,128]{1,0:T(8,128)(2,1)} custom-call(bf16[128,128]{1,0:T(8,128)(2,1)} %reshape.103.q_ref, bf16[16,128,66]{2,1,0:T(8,128)(2,1)} %bitcast.55, bf16[16896,256]{1,0:T(8,128)(2,1)} %bitcast.46), custom_call_target="tpu_custom_call" | custom-call | flops 1107296256 | bytes 8650752 | tf_op jit(solution)/shard_map/pool_attention/pallas_call | solution.py:69
  27.3 0.8 reshape.105
  28.1 3.1 %convolution_convert_fusion.1 = bf16[32,4096]{1,0:T(8,128)(2,1)S(1)} fusion(bf16[32,512]{1,0:T(8,128)(2,1)S(1)} %reshape.105, bf16[512,4096]{1,0:T(8,128)(2,1)} %param.22), kind=kOutput, calls=%fused_computation.3 | convolution fusion | flops 134348800 | bytes 4489216 | tf_op jit(solution)/shard_map/dot_general | solution.py:335
  31.2 0.8 reshape.106
  32.0 5.9 %all-to-all-start = ((bf16[8,4,4096]{2,1,0:T(4,128)(2,1)}), bf16[8,4,4096]{2,1,0:T(4,128)(2,1)S(1)}, u32[]{:S(2)}, u32[]{:S(2)}) async-start(bf16[8,4,4096]{2,1,0:T(4,128)(2,1)} %reshape.106), calls=%async_computation | async-start | bytes 524288 | tf_op jit(solution)/shard_map/all_to_all | solution.py:336
  38.0 0.1 select_reduce_fusion.3
  38.3 0.1 eq.94
  38.6 0.2 reduce_window_sum.11
  38.7 0.2 select_reduce_fusion.1
  38.9 0.1 reduce_sum.61
  39.4 6.0 %all-to-all-done = bf16[8,4,4096]{2,1,0:T(4,128)(2,1)S(1)} async-done(((bf16[8,4,4096]{2,1,0:T(4,128)(2,1)}), bf16[8,4,4096]{2,1,0:T(4,128)(2,1)S(1)}, u32[]{:S(2)}, u32[]{:S(2)}) %all-to-all-start) | async-done | bytes 262176 | tf_op jit(solution)/shard_map/all_to_all | solution.py:336
  45.5 0.1 convert_reduce_fusion
  45.6 0.2 fusion.4
  45.9 0.4 copy-done.3
  46.2 0.5 fusion
  46.8 1.3 copy.26
  48.1 38.3 %plane_send.1 = bf16[16,18,32,128]{3,2,1,0:T(8,128)(2,1)} custom-call(bf16[8,18,32,128]{3,2,1,0:T(8,128)(2,1)} %bitcast.48), custom_call_target="tpu_custom_call" | custom-call | tf_op jit(solution)/shard_map/plane_send/pallas_call | solution.py:142
  86.4 4.2 %copy.36 = bf16[36,8,32,128]{3,1,2,0:T(8,128)(2,1)} copy(bf16[36,8,32,128]{3,2,1,0:T(8,128)(2,1)} %bitcast.44) | data formatting | bytes 4718592
  90.7 158.2 %expert_exchange.1 = bf16[288,4096]{1,0:T(8,128)(2,1)} custom-call(bf16[288,4096]{1,0:T(8,128)(2,1)} %bitcast.42, bf16[4096,512]{1,0:T(8,128)(2,1)} %bitcast.50, bf16[4096,512]{1,0:T(8,128)(2,1)} %collective-permute-done.gate1, bf16[4096,512]{1,0:T(8,128)(2,1)} %bitcast.52, bf16[4096,512]{1,0:T(8,128)(2,1)} %collective-permute-done.1.up1, ...), custom_call_target="tpu_custom_call" | custom-call | tf_op jit(solution)/shard_map/expert_exchange/pallas_call | solution.py:285
  248.9 3.6 %copy.28 = bf16[36,8,32,128]{3,2,1,0:T(8,128)(2,1)} copy(bf16[36,8,32,128]{3,1,2,0:T(8,128)(2,1)} %bitcast.43) | data formatting | bytes 4718592
  252.5 39.8 %plane_return.1 = bf16[16,18,32,128]{3,2,1,0:T(8,128)(2,1)} custom-call(bf16[16,18,32,128]{3,2,1,0:T(8,128)(2,1)} %bitcast.45), custom_call_target="tpu_custom_call" | custom-call | tf_op jit(solution)/shard_map/plane_return/pallas_call | solution.py:142
  292.3 1.9 add_convert_fusion
  294.3 0.6 fusion.1
  294.8 0.4 copy-done.1
  295.3 0.3 fusion.8
  295.6 0.7 slice_bitcast_fusion
  (44 shorter events, 1.2 us)
Async XLA Ops:
  0.6 9.1 %copy-start.5 = (bf16[32,512]{1,0:T(8,128)(2,1)S(1)}, bf16[32,512]{1,0:T(8,128)(2,1)}, u32[]{:S(2)}) copy-start(bf16[32,512]{1,0:T(8,128)(2,1)} %param.18) | copy-start | bytes 98308
  0.6 90.0 %collective-permute-start = (bf16[4096,512]{1,0:T(8,128)(2,1)}, bf16[4096,512]{1,0:T(8,128)(2,1)}, u32[]{:S(2)}, u32[]{:S(2)}) collective-permute-start(bf16[4096,512]{1,0:T(8,128)(2,1)} %bitcast.49), channel_id=1, source_target_pairs={{0,1},{1,0},{2,3},{3,2},{4,5},{5,4},{6,7},{7,6},{8,9},{9,8},{10,11... | collective-permute-start | bytes 12582920 | tf_op jit(solution)/shard_map/ppermute | solution.py:331
  0.7 89.9 %collective-permute-start.1 = (bf16[4096,512]{1,0:T(8,128)(2,1)}, bf16[4096,512]{1,0:T(8,128)(2,1)}, u32[]{:S(2)}, u32[]{:S(2)}) collective-permute-start(bf16[4096,512]{1,0:T(8,128)(2,1)} %bitcast.51), channel_id=1, source_target_pairs={{0,1},{1,0},{2,3},{3,2},{4,5},{5,4},{6,7},{7,6},{8,9},{9,8},{10,11... | collective-permute-start | bytes 12582920 | tf_op jit(solution)/shard_map/ppermute | solution.py:332
  1.2 89.4 %collective-permute-start.2 = (bf16[512,4096]{1,0:T(8,128)(2,1)}, bf16[512,4096]{1,0:T(8,128)(2,1)}, u32[]{:S(2)}, u32[]{:S(2)}) collective-permute-start(bf16[512,4096]{1,0:T(8,128)(2,1)} %bitcast.53), channel_id=1, source_target_pairs={{0,1},{1,0},{2,3},{3,2},{4,5},{5,4},{6,7},{7,6},{8,9},{9,8},{10,11... | collective-permute-start | bytes 12582920 | tf_op jit(solution)/shard_map/ppermute | solution.py:333
  28.0 9.9 %copy-start.8 = (s32[1,4,2]{1,2,0:T(2,128)S(1)}, s32[1,4,2]{1,2,0:T(2,128)}, u32[]{:S(2)}) copy-start(s32[1,4,2]{1,2,0:T(2,128)} %param.25) | copy-start | bytes 100
  28.1 9.9 %copy-start.9 = (s32[60,2]{0,1:T(2,128)S(1)}, s32[60,2]{0,1:T(2,128)}, u32[]{:S(2)}) copy-start(s32[60,2]{0,1:T(2,128)} %param.24) | copy-start | bytes 1444
  28.1 10.0 %copy-start.12 = (s32[8]{0:T(128)S(1)}, s32[8]{0:T(128)}, u32[]{:S(2)}) copy-start(s32[8]{0:T(128)} %param.28) | copy-start | bytes 100
  28.1 11.2 %copy-start.10 = (f32[1,4,2]{1,2,0:T(2,128)S(1)}, f32[1,4,2]{1,2,0:T(2,128)}, u32[]{:S(2)}) copy-start(f32[1,4,2]{1,2,0:T(2,128)} %param.27) | copy-start | bytes 100
  28.1 11.2 %copy-start.11 = (f32[60,2]{0,1:T(2,128)S(1)}, f32[60,2]{0,1:T(2,128)}, u32[]{:S(2)}) copy-start(f32[60,2]{0,1:T(2,128)} %param.26) | copy-start | bytes 1444
  28.1 17.5 %copy-start.6 = (bf16[1,4,4096]{2,1,0:T(4,128)(2,1)S(1)}, bf16[1,4,4096]{2,1,0:T(4,128)(2,1)}, u32[]{:S(2)}) copy-start(bf16[1,4,4096]{2,1,0:T(4,128)(2,1)} %param.17) | copy-start | bytes 98308
  28.1 17.5 %copy-start = (bf16[60,4096]{1,0:T(8,128)(2,1)S(1)}, bf16[60,4096]{1,0:T(8,128)(2,1)}, u32[]{:S(2)}) copy-start(bf16[60,4096]{1,0:T(8,128)(2,1)} %param.16) | copy-start | bytes 1474564
  31.2 15.0 %copy-start.7 = (f32[4096]{0:T(1024)S(1)}, f32[4096]{0:T(1024)}, u32[]{:S(2)}) copy-start(f32[4096]{0:T(1024)} %param.23) | copy-start | bytes 49156
  32.0 13.4 %all-to-all-start = ((bf16[8,4,4096]{2,1,0:T(4,128)(2,1)}), bf16[8,4,4096]{2,1,0:T(4,128)(2,1)S(1)}, u32[]{:S(2)}, u32[]{:S(2)}) async-start(bf16[8,4,4096]{2,1,0:T(4,128)(2,1)} %reshape.106), calls=%async_computation | async-start | bytes 524288 | tf_op jit(solution)/shard_map/all_to_all | solution.py:336
  45.6 0.6 copy-start.3
  294.2 1.0 copy-start.1
  294.3 1.0 copy-start.4
  295.6 0.8 copy-start.2

commit v2 on v1

--- a/solution.py
+++ b/solution.py
@@ -11,6 +11,8 @@
 Z_HALVES = 2
 SHARD_PLANE = X_CHIPS * CORES
 LOWEST = -1e30
+BLOCK = 16
+CHUNKS = 3
 
 
 def attention_kernel(q_ref, count_ref, kv_ref, out_ref, top, total, summed):
@@ -155,34 +157,76 @@
 
 
 def expert_kernel(
-    rows_ref, gate0, gate1, up0, up1, down0, down1, out_ref,
-    held, partial, direct, relayed, act, gate, up, down,
-    send_sem, recv_sem, load_sem,
+    blocks_ref, rest_ref, gate0, gate1, up0, up1, down0, down1, back_ref, rest_out,
+    rows, held, partial, direct, relayed, sums, act, gate, up, down,
+    plane_send, plane_recv, back_send, back_recv, send_sem, recv_sem, load_sem,
 ):
     expert = lax.axis_index("expert")
     shard = lax.axis_index("shard")
+    n_expert, block, width = blocks_ref.shape
     half, rest = shard // SHARD_PLANE, shard % SHARD_PLANE
     chip, core = rest // CORES, rest % CORES
     right = half * SHARD_PLANE + (chip + 1) % X_CHIPS * CORES + core
     left = half * SHARD_PLANE + (chip + X_CHIPS - 1) % X_CHIPS * CORES + core
-    count = rows_ref.shape[0]
+    mine = half * n_expert + expert
+    peers = Z_HALVES * n_expert
+    count = rows.shape[0]
     part = count // 2
-    low, high = pl.ds(0, part), pl.ds(part, part)
-
-    loads = []
-    for at, (src, dst) in enumerate(
-        ((gate0, gate.at[0]), (up0, up.at[0]), (gate1, gate.at[1]), (up1, up.at[1]), (down0, down.at[0]), (down1, down.at[1]))
-    ):
-        load = pltpu.make_async_copy(src, dst, load_sem.at[at])
-        load.start()
-        loads.append(load)
+    chunk = part // CHUNKS
+    main = n_expert * block
+
+    def ahead(step):
+        to_half = (half + step // n_expert) % Z_HALVES
+        return (expert + step) % n_expert, to_half * SHARD_PLANE + rest
+
+    def behind(step):
+        to_half = (half + step // n_expert) % Z_HALVES
+        return (expert + n_expert - step % n_expert) % n_expert, to_half * SHARD_PLANE + rest
+
+    def lines_of(step):
+        return pl.ds(step // n_expert * part + step % n_expert * block, block)
+
+    def local_copy(at, src, dst):
+        copy = pltpu.make_async_copy(src, dst, load_sem.at[at])
+        copy.start()
+        return copy
+
+    own = local_copy(6, blocks_ref.at[expert], rows.at[lines_of(0)])
+    rests = [
+        local_copy(7 + side, rest_ref.at[pl.ds(side * block, block)], rows.at[pl.ds(side * part + main, block)])
+        for side in range(2)
+    ]
+    loads = [
+        local_copy(at, src, dst)
+        for at, (src, dst) in enumerate(
+            ((gate0, gate.at[0]), (up0, up.at[0]), (gate1, gate.at[1]), (up1, up.at[1]), (down0, down.at[0]), (down1, down.at[1]))
+        )
+    ]
 
     barrier = pltpu.get_barrier_semaphore()
     for neighbour in (left, right):
         pl.semaphore_signal(barrier, inc=1, device_id=(expert, neighbour), device_id_type=MESH)
-    pl.semaphore_wait(barrier, 2)
-
-    def send(at, src, dst, to):
+    for step in range(1, peers):
+        pl.semaphore_signal(barrier, inc=1, device_id=ahead(step), device_id_type=MESH)
+    pl.semaphore_wait(barrier, peers + 1)
+
+    spread = []
+    for step in range(1, peers):
+        copy = pltpu.make_async_remote_copy(
+            src_ref=blocks_ref.at[ahead(step)[0]],
+            dst_ref=rows.at[lines_of(step)],
+            send_sem=plane_send.at[step],
+            recv_sem=plane_recv.at[step],
+            device_id=ahead(step),
+            device_id_type=MESH,
+        )
+        copy.start()
+        spread.append(copy)
+
+    sent = []
+
+    def send(src, dst, to):
+        at = len(sent)
         copy = pltpu.make_async_remote_copy(
             src_ref=src,
             dst_ref=dst,
@@ -192,16 +236,27 @@
             device_id_type=MESH,
         )
         copy.start()
+        sent.append(copy)
         return copy
 
-    first_r = send(0, rows_ref.at[low], held.at[0, low], right)
-    first_l = send(1, rows_ref.at[high], held.at[0, high], left)
-    second_r = send(2, rows_ref.at[high], held.at[1, high], right)
-    second_l = send(3, rows_ref.at[low], held.at[1, low], left)
+    near = [[], []]
+    later = []
+
+    def forward(lines, side):
+        near[side].append(send(rows.at[lines], held.at[side, lines], right))
+        later.append(send(rows.at[lines], held.at[1 - side, lines], left))
+
+    for side in range(2):
+        rests[side].wait()
+        forward(pl.ds(side * part + main, block), side)
+    own.wait()
+    forward(lines_of(0), 0)
+    for step in range(1, peers):
+        spread[step - 1].wait_recv()
+        forward(lines_of(step), step // n_expert)
     for load in loads:
         load.wait()
 
-    width = rows_ref.shape[1]
     ff = gate.shape[2]
     tile = 256
     wide = 512
@@ -222,89 +277,133 @@
             o = o + jnp.dot(act[1], down[1, :, columns], preferred_element_type=jnp.float32)
             dst[:, columns] = o.astype(dst.dtype)
 
-    feed_forward(rows_ref, partial.at[3])
-    first_r.wait_recv()
-    third_r = send(4, held.at[0, low], held.at[2, low], right)
-    first_l.wait_recv()
-    third_l = send(5, held.at[0, high], held.at[2, high], left)
+    def piece(side, c):
+        return pl.ds(side * part + c * chunk, chunk)
+
+    feed_forward(rows, partial.at[3])
+    for copy in near[0] + near[1] + later:
+        copy.wait_recv()
+    third = []
+    for c in range(CHUNKS):
+        third.append(send(held.at[0, piece(0, c)], held.at[2, piece(0, c)], right))
+        third.append(send(held.at[0, piece(1, c)], held.at[2, piece(1, c)], left))
     feed_forward(held.at[0], partial.at[0])
-    plain_r = send(6, partial.at[0, high], direct.at[0, high], right)
-    plain_l = send(7, partial.at[0, low], direct.at[1, low], left)
-    second_r.wait_recv()
-    second_l.wait_recv()
-    feed_forward(held.at[1], partial.at[1])
-    third_r.wait_recv()
-    third_l.wait_recv()
-    feed_forward(held.at[2], partial.at[2])
-    far_r = send(8, partial.at[2, low], relayed.at[low], right)
-    far_l = send(9, partial.at[2, high], relayed.at[high], left)
-
-    strip = 48
-
-    def add_relayed(start):
-        @pl.loop(0, part // strip)
-        def _(t):
-            lines = pl.ds(pl.multiple_of(start + t * strip, 16), strip)
+
+    def send_plain(c):
+        return (
+            send(partial.at[0, piece(1, c)], direct.at[0, piece(1, c)], right),
+            send(partial.at[0, piece(0, c)], direct.at[1, piece(0, c)], left),
+        )
+
+    def send_far(c):
+        return (
+            send(partial.at[2, piece(0, c)], relayed.at[piece(0, c)], right),
+            send(partial.at[2, piece(1, c)], relayed.at[piece(1, c)], left),
+        )
+
+    def send_joined(c, far):
+        joined = []
+        for side, to in ((0, right), (1, left)):
+            far[side].wait_recv()
+            lines = piece(side, c)
             partial[1, lines, :] = (
                 partial[1, lines, :].astype(jnp.float32) + relayed[lines, :].astype(jnp.float32)
             ).astype(partial.dtype)
-
-    far_r.wait_recv()
-    add_relayed(0)
-    joined_r = send(10, partial.at[1, low], direct.at[0, low], right)
-    far_l.wait_recv()
-    add_relayed(part)
-    joined_l = send(11, partial.at[1, high], direct.at[1, high], left)
-    plain_r.wait_recv()
-    plain_l.wait_recv()
-    joined_r.wait_recv()
-    joined_l.wait_recv()
-
-    @pl.loop(0, count // strip)
-    def _(t):
-        lines = pl.ds(pl.multiple_of(t * strip, 16), strip)
-        out_ref[lines, :] = (
-            partial[3, lines, :].astype(jnp.float32)
-            + direct[0, lines, :].astype(jnp.float32)
-            + direct[1, lines, :].astype(jnp.float32)
-        ).astype(out_ref.dtype)
-
-    for copy in (
-        first_r, first_l, second_r, second_l, third_r, third_l,
-        plain_r, plain_l, far_r, far_l, joined_r, joined_l,
-    ):
+            joined.append(send(partial.at[1, lines], direct.at[side, lines], to))
+        return joined
+
+    plain = [send_plain(0), send_plain(1)]
+    feed_forward(held.at[1], partial.at[1])
+    for copy in third:
+        copy.wait_recv()
+    feed_forward(held.at[2], partial.at[2])
+    far = [send_far(0), send_far(1)]
+    joined = [send_joined(0, far[0])]
+    far.append(send_far(2))
+    joined.append(send_joined(1, far[1]))
+    plain.append(send_plain(2))
+    joined.append(send_joined(2, far[2]))
+
+    returns = []
+    locals_ = []
+    for c in range(CHUNKS):
+        for copy in (*plain[c], *joined[c]):
+            copy.wait_recv()
+        for side in range(2):
+            lines = piece(side, c)
+            sums[lines, :] = (
+                partial[3, lines, :].astype(jnp.float32)
+                + direct[0, lines, :].astype(jnp.float32)
+                + direct[1, lines, :].astype(jnp.float32)
+            ).astype(sums.dtype)
+        for at in range(c * chunk // block, (c + 1) * chunk // block):
+            for side in range(2):
+                step = side * n_expert + at
+                if at == n_expert:
+                    locals_.append(
+                        local_copy(7 + side, sums.at[pl.ds(side * part + main, block)], rest_out.at[pl.ds(side * block, block)])
+                    )
+                elif step == 0:
+                    locals_.append(local_copy(6, sums.at[lines_of(0)], back_ref.at[mine]))
+                else:
+                    copy = pltpu.make_async_remote_copy(
+                        src_ref=sums.at[lines_of(step)],
+                        dst_ref=back_ref.at[mine],
+                        send_sem=back_send.at[step],
+                        recv_sem=back_recv.at[step],
+                        device_id=behind(step),
+                        device_id_type=MESH,
+                    )
+                    copy.start()
+                    returns.append(copy)
+    for copy in locals_:
+        copy.wait()
+    for copy in returns:
+        copy.wait()
+    for copy in spread + sent:
         copy.wait_send()
 
 
-def expert_exchange(rows, gates, ups, downs, collective_id):
-    count, width = rows.shape
+def expert_exchange(blocks, rest, gates, ups, downs, collective_id):
+    n_expert, block, width = blocks.shape
+    peers = Z_HALVES * n_expert
     ff = gates[0].shape[1]
     bf16 = jnp.bfloat16
-    vmem = pl.BlockSpec(memory_space=pltpu.VMEM)
+    count = peers * block + rest.shape[0]
     anywhere = pl.BlockSpec(memory_space=pl.ANY)
+    sends = 2 * (peers + 2) + 8 * CHUNKS
     return pl.pallas_call(
         expert_kernel,
-        out_shape=jax.ShapeDtypeStruct((count, width), bf16),
-        in_specs=[vmem] + [anywhere] * 6,
-        out_specs=vmem,
+        out_shape=(
+            jax.ShapeDtypeStruct((peers, block, width), bf16),
+            jax.ShapeDtypeStruct(rest.shape, bf16),
+        ),
+        in_specs=[anywhere] * 8,
+        out_specs=(anywhere, anywhere),
         scratch_shapes=[
+            pltpu.VMEM((count, width), bf16),
             pltpu.VMEM((3, count, width), bf16),
             pltpu.VMEM((4, count, width), bf16),
             pltpu.VMEM((2, count, width), bf16),
+            pltpu.VMEM((count, width), bf16),
             pltpu.VMEM((count, width), bf16),
             pltpu.VMEM((2, count, ff), bf16),
             pltpu.VMEM((2, width, ff), bf16),
             pltpu.VMEM((2, width, ff), bf16),
             pltpu.VMEM((2, ff, width), bf16),
-            pltpu.SemaphoreType.DMA((12,)),
-            pltpu.SemaphoreType.DMA((12,)),
-            pltpu.SemaphoreType.DMA((6,)),
+            pltpu.SemaphoreType.DMA((peers,)),
+            pltpu.SemaphoreType.DMA((peers,)),
+            pltpu.SemaphoreType.DMA((peers,)),
+            pltpu.SemaphoreType.DMA((peers,)),
+            pltpu.SemaphoreType.DMA((sends,)),
+            pltpu.SemaphoreType.DMA((sends,)),
+            pltpu.SemaphoreType.DMA((9,)),
         ],
         compiler_params=pltpu.CompilerParams(
             collective_id=collective_id, has_side_effects=True, vmem_limit_bytes=66 * 1024 * 1000 - 560000
         ),
         name="expert_exchange",
-    )(rows, *gates, *ups, *downs)
+    )(blocks, rest, *gates, *ups, *downs)
 
 
 def local(
@@ -360,24 +459,38 @@
     flat_slots = slot_ids.reshape(-1)
     slot_hot = (flat_slots[:, None] == expert_ids[None, :]).astype(jnp.int32)
     ranking = jnp.sum((jnp.cumsum(slot_hot, axis=0) - slot_hot) * slot_hot, axis=1)
-    slot_pos = (flat_slots * slot_cap + ranking).reshape(rows_dev, 2)
+    rest_cap = slot_cap - BLOCK
+    main_all = experts * BLOCK
     slots_all = experts * slot_cap
+    slot_pos = jnp.where(
+        ranking < BLOCK, flat_slots * BLOCK + ranking, main_all + flat_slots * rest_cap + ranking - BLOCK
+    ).reshape(rows_dev, 2)
     chosen = jnp.arange(slots_all, dtype=jnp.int32)[:, None, None] == slot_pos[None]
     placing = jnp.any(chosen, axis=-1).astype(jnp.bfloat16)
-    buffer = jnp.dot(placing, normed, preferred_element_type=jnp.float32).astype(jnp.bfloat16)
     lanes = 128
-    buffer = buffer.reshape(experts, slot_cap, width // lanes, lanes)
-    received = plane_exchange(buffer, n_expert, False, 0)
-    rows = received.reshape(-1, width)
-    sums = expert_exchange(rows, gates, ups, downs, 1)
-    returned = plane_exchange(
-        sums.reshape(Z_HALVES * n_expert, slot_cap, width // lanes, lanes), n_expert, True, 2
-    ).reshape(Z_HALVES, slots_all, width)
-    outputs = (returned[0].astype(jnp.float32) + returned[1].astype(jnp.float32)).astype(jnp.bfloat16)
+    blocks = jnp.dot(placing[:main_all], normed, preferred_element_type=jnp.float32).astype(jnp.bfloat16)
+    rest = jnp.dot(placing[main_all:], normed, preferred_element_type=jnp.float32).astype(jnp.bfloat16)
+    rest_in = plane_exchange(
+        rest.reshape(experts, rest_cap, width // lanes, lanes), n_expert, False, 0
+    ).reshape(-1, width)
+    back, rest_sums = expert_exchange(
+        blocks.reshape(experts, BLOCK, width), rest_in, gates, ups, downs, 1
+    )
+    rest_back = plane_exchange(
+        rest_sums.reshape(Z_HALVES * n_expert, rest_cap, width // lanes, lanes), n_expert, True, 2
+    ).reshape(Z_HALVES, experts * rest_cap, width)
+    back = back.reshape(Z_HALVES, main_all, width)
     picking = (slot_pos.T.reshape(-1)[:, None] == jnp.arange(slots_all, dtype=jnp.int32)[None, :]).astype(
         jnp.bfloat16
     )
-    picked = jnp.dot(picking, outputs, preferred_element_type=jnp.float32).reshape(2, rows_dev, width)
+
+    def pick(mask, halves):
+        outputs = (halves[0].astype(jnp.float32) + halves[1].astype(jnp.float32)).astype(jnp.bfloat16)
+        return jnp.dot(mask, outputs, preferred_element_type=jnp.float32)
+
+    picked = (pick(picking[:, :main_all], back) + pick(picking[:, main_all:], rest_back)).reshape(
+        2, rows_dev, width
+    )
     mixed_rows = stream + shares[:, :1] * picked[0] + shares[:, 1:] * picked[1]
     mixed_out = mixed_rows.astype(jnp.bfloat16)
     return (mixed_out[:pre_count], mixed_out[pre_count:][None])

time: 299 us -> 257 us (0.86)
  Pallas kernels: 253 us -> 216 us
  local copies, waits for them, and re-layouts: 15.6 us -> 10.6 us
    pallas_call x2, Pallas kernels: 78.1 us -> 20 us  [plane_exchange(): pl.pallas_call(kernel, out_shape=jax.ShapeDtypeStruct((peers,) + block, b...]
    pallas_call x1, Pallas kernels: 158 us -> 179 us  [expert_exchange(): pl.pallas_call(expert_kernel, out_shape=(jax.ShapeDtypeStruct((peers, blo...]
    unnamed x29, local copies, waits for them, and re-layouts: 10.1 us -> 4.29 us
  transfers between devices with their start and end apart: 4 -> 4, of which waited for: 1 -> 1; matrix products, arithmetic and copies ran while one was open for 7% -> 8% of each run, Pallas kernels for 19% -> 11%
where the time goes in v2:
time: 257 us; the launch traced here: 256 us
  Pallas kernels  216 us (84%)
  other arithmetic  11.5 us (4%)
  local copies, waits for them, and re-layouts  10.6 us (4%)
  starting transfers between devices  6.59 us (3%)
  matrix products  5.66 us (2%)
  waiting for transfers between devices  5.31 us (2%)
    pallas_call x1, Pallas kernels, expert_exchange(): pl.pallas_call(expert_kernel, out_shape=(jax.ShapeDtypeStruct((peers, blo...  179 us
    pallas_call x2, Pallas kernels, plane_exchange(): pl.pallas_call(kernel, out_shape=jax.ShapeDtypeStruct((peers,) + block, b...  20 us
    pallas_call x1, Pallas kernels, pool_attention(): pl.pallas_call(attention_kernel, grid=(steps,), in_specs=[pl.BlockSpec((r...  16.9 us
    all_to_all x1, starting transfers between devices, local(): lax.all_to_all(head_part.reshape(n_expert, -1, head_part.shape[1]), 'expe...  5.91 us
    reduce_sum x1, other arithmetic, pool_attention(): jnp.sum(jnp.where(page_rows[:, :, None] == pool_ids[None, None, :], in_pa...  5.66 us
    all_to_all x1, waiting for transfers between devices, local(): lax.all_to_all(head_part.reshape(n_expert, -1, head_part.shape[1]), 'expe...  5.3 us
  transfers between devices with their start and end apart: 4, of which 1 were waited for; matrix products, arithmetic and copies ran while one was open for 8% of the time, Pallas kernels for 11%

profile of v2, /device:TPU:0, one launch (start us, length us, event | category | flops | bytes accessed | tf_op | source)
XLA Modules:
  0.0 256.5 jit_solution(17840756523852329097)
XLA Ops:
  0.7 0.5 collective-permute-start.1
  1.3 0.7 subtract_clamp_fusion
  2.0 5.7 %select_reduce_fusion = s32[32,1056]{1,0:T(8,128)S(1)} fusion(s32[32,128]{1,0:T(8,128)S(1)} %subtract_clamp_fusion, s32[32,128]{1,0:T(8,128)} %bitcast.61), kind=kLoop, calls=%fused_computation | loop fusion | flops 12942336 | bytes 167936 | tf_op jit(solution)/shard_map/reduce_sum | solution.py:66
  7.8 0.9 reshape_reshape.3
  8.8 0.9 copy.38
  9.7 1.4 reshape.127.q_ref
  11.1 16.9 %pool_attention.1 = bf16[128,128]{1,0:T(8,128)(2,1)} custom-call(bf16[128,128]{1,0:T(8,128)(2,1)} %reshape.127.q_ref, bf16[16,128,66]{2,1,0:T(8,128)(2,1)} %bitcast.53, bf16[16896,256]{1,0:T(8,128)(2,1)} %bitcast.44), custom_call_target="tpu_custom_call" | custom-call | flops 1107296256 | bytes 8650752 | tf_op jit(solution)/shard_map/pool_attention/pallas_call | solution.py:71
  28.1 0.8 reshape.129
  28.9 3.0 %convolution_convert_fusion.1 = bf16[32,4096]{1,0:T(8,128)(2,1)S(1)} fusion(bf16[32,512]{1,0:T(8,128)(2,1)S(1)} %reshape.129, bf16[512,4096]{1,0:T(8,128)(2,1)} %param.22), kind=kOutput, calls=%fused_computation.4 | convolution fusion | flops 134348800 | bytes 4489216 | tf_op jit(solution)/shard_map/dot_general | solution.py:434
  31.9 0.8 reshape.130
  32.7 5.9 %all-to-all-start = ((bf16[8,4,4096]{2,1,0:T(4,128)(2,1)}), bf16[8,4,4096]{2,1,0:T(4,128)(2,1)S(1)}, u32[]{:S(2)}, u32[]{:S(2)}) async-start(bf16[8,4,4096]{2,1,0:T(4,128)(2,1)} %reshape.130), calls=%async_computation | async-start | bytes 524288 | tf_op jit(solution)/shard_map/all_to_all | solution.py:435
  39.1 0.1 eq.94
  39.3 0.2 reduce_window_sum.11
  39.5 0.2 select_reduce_fusion.1
  39.6 0.1 reduce_sum.61
  40.2 0.7 iota_compare_fusion.2
  40.9 5.3 %all-to-all-done = bf16[8,4,4096]{2,1,0:T(4,128)(2,1)S(1)} async-done(((bf16[8,4,4096]{2,1,0:T(4,128)(2,1)}), bf16[8,4,4096]{2,1,0:T(4,128)(2,1)S(1)}, u32[]{:S(2)}, u32[]{:S(2)}) %all-to-all-start) | async-done | bytes 262176 | tf_op jit(solution)/shard_map/all_to_all | solution.py:435
  46.3 0.2 fusion.1
  46.6 0.3 fusion
  46.9 0.7 copy.28
  47.6 10.6 %plane_send.1 = bf16[16,2,32,128]{3,2,1,0:T(8,128)(2,1)} custom-call(bf16[8,2,32,128]{3,2,1,0:T(8,128)(2,1)} %bitcast.59), custom_call_target="tpu_custom_call" | custom-call | tf_op jit(solution)/shard_map/plane_send/pallas_call | solution.py:144
  58.2 1.8 copy.39
  59.9 1.5 convolution_convert_fusion
  61.4 179.1 %expert_exchange.1 = (bf16[16,16,4096]{2,1,0:T(8,128)(2,1)}, bf16[32,4096]{1,0:T(8,128)(2,1)}) custom-call(bf16[8,16,4096]{2,1,0:T(8,128)(2,1)} %bitcast.52, bf16[32,4096]{1,0:T(8,128)(2,1)} %bitcast.54, bf16[4096,512]{1,0:T(8,128)(2,1)} %bitcast.46, bf16[4096,512]{1,0:T(8,128)(2,1)} %collective-permute-done.gate1, bf16[4096,512]{1,0:T(8,128)(2,1)} %bitcast.48, ...), custom_call_target="tpu_custom_call" | custom-call | tf_op jit(solution)/shard_map/expert_exchange/pallas_call | solution.py:375
  240.6 1.8 add_convert_fusion
  242.4 1.7 copy.30
  244.1 9.4 %plane_return.1 = bf16[16,2,32,128]{3,2,1,0:T(8,128)(2,1)} custom-call(bf16[16,2,32,128]{3,2,1,0:T(8,128)(2,1)} %bitcast.56), custom_call_target="tpu_custom_call" | custom-call | tf_op jit(solution)/shard_map/plane_return/pallas_call | solution.py:144
  253.4 1.0 add_convert_fusion.1
  254.5 0.4 fusion.14
  254.9 0.4 convolution_add_fusion
  255.3 0.3 fusion.5
  255.7 0.7 slice_bitcast_fusion
  (48 shorter events, 1.4 us)
Async XLA Ops:
  0.6 60.8 %collective-permute-start = (bf16[4096,512]{1,0:T(8,128)(2,1)}, bf16[4096,512]{1,0:T(8,128)(2,1)}, u32[]{:S(2)}, u32[]{:S(2)}) collective-permute-start(bf16[4096,512]{1,0:T(8,128)(2,1)} %bitcast.45), channel_id=1, source_target_pairs={{0,1},{1,0},{2,3},{3,2},{4,5},{5,4},{6,7},{7,6},{8,9},{9,8},{10,11... | collective-permute-start | bytes 12582920 | tf_op jit(solution)/shard_map/ppermute | solution.py:430
  0.7 60.7 %collective-permute-start.1 = (bf16[4096,512]{1,0:T(8,128)(2,1)}, bf16[4096,512]{1,0:T(8,128)(2,1)}, u32[]{:S(2)}, u32[]{:S(2)}) collective-permute-start(bf16[4096,512]{1,0:T(8,128)(2,1)} %bitcast.47), channel_id=1, source_target_pairs={{0,1},{1,0},{2,3},{3,2},{4,5},{5,4},{6,7},{7,6},{8,9},{9,8},{10,11... | collective-permute-start | bytes 12582920 | tf_op jit(solution)/shard_map/ppermute | solution.py:431
  1.2 60.2 %collective-permute-start.2 = (bf16[512,4096]{1,0:T(8,128)(2,1)}, bf16[512,4096]{1,0:T(8,128)(2,1)}, u32[]{:S(2)}, u32[]{:S(2)}) collective-permute-start(bf16[512,4096]{1,0:T(8,128)(2,1)} %bitcast.49), channel_id=1, source_target_pairs={{0,1},{1,0},{2,3},{3,2},{4,5},{5,4},{6,7},{7,6},{8,9},{9,8},{10,11... | collective-permute-start | bytes 12582920 | tf_op jit(solution)/shard_map/ppermute | solution.py:432
  28.0 10.7 %copy-start.8 = (s32[1,4,2]{1,2,0:T(2,128)S(1)}, s32[1,4,2]{1,2,0:T(2,128)}, u32[]{:S(2)}) copy-start(s32[1,4,2]{1,2,0:T(2,128)} %param.25) | copy-start | bytes 100
  28.0 10.7 %copy-start.9 = (s32[60,2]{0,1:T(2,128)S(1)}, s32[60,2]{0,1:T(2,128)}, u32[]{:S(2)}) copy-start(s32[60,2]{0,1:T(2,128)} %param.24) | copy-start | bytes 1444
  28.0 10.7 %copy-start.12 = (s32[8]{0:T(128)S(1)}, s32[8]{0:T(128)}, u32[]{:S(2)}) copy-start(s32[8]{0:T(128)} %param.28) | copy-start | bytes 100
  28.0 11.9 %copy-start.10 = (f32[1,4,2]{1,2,0:T(2,128)S(1)}, f32[1,4,2]{1,2,0:T(2,128)}, u32[]{:S(2)}) copy-start(f32[1,4,2]{1,2,0:T(2,128)} %param.27) | copy-start | bytes 100
  28.0 11.8 %copy-start.11 = (f32[60,2]{0,1:T(2,128)S(1)}, f32[60,2]{0,1:T(2,128)}, u32[]{:S(2)}) copy-start(f32[60,2]{0,1:T(2,128)} %param.26) | copy-start | bytes 1444
  28.0 18.3 %copy-start.6 = (bf16[1,4,4096]{2,1,0:T(4,128)(2,1)S(1)}, bf16[1,4,4096]{2,1,0:T(4,128)(2,1)}, u32[]{:S(2)}) copy-start(bf16[1,4,4096]{2,1,0:T(4,128)(2,1)} %param.17) | copy-start | bytes 98308
  28.0 18.3 %copy-start = (bf16[60,4096]{1,0:T(8,128)(2,1)S(1)}, bf16[60,4096]{1,0:T(8,128)(2,1)}, u32[]{:S(2)}) copy-start(bf16[60,4096]{1,0:T(8,128)(2,1)} %param.16) | copy-start | bytes 1474564
  28.1 18.5 %copy-start.7 = (f32[4096]{0:T(1024)S(1)}, f32[4096]{0:T(1024)}, u32[]{:S(2)}) copy-start(f32[4096]{0:T(1024)} %param.23) | copy-start | bytes 49156
  32.7 13.4 %all-to-all-start = ((bf16[8,4,4096]{2,1,0:T(4,128)(2,1)}), bf16[8,4,4096]{2,1,0:T(4,128)(2,1)S(1)}, u32[]{:S(2)}, u32[]{:S(2)}) async-start(bf16[8,4,4096]{2,1,0:T(4,128)(2,1)} %reshape.130), calls=%async_computation | async-start | bytes 524288 | tf_op jit(solution)/shard_map/all_to_all | solution.py:435
  46.3 15.1 %copy-start.3 = (bf16[4,4096]{1,0:T(4,128)(2,1)}, bf16[4,4096]{1,0:T(4,128)(2,1)S(1)}, u32[]{:S(2)}) copy-start(bf16[4,4096]{1,0:T(4,128)(2,1)S(1)} %fusion.11) | copy-start | bytes 98308
  240.5 13.9 %copy-start.5 = (pred[128,144]{1,0:T(32,128)(4,1)S(1)}, pred[128,144]{1,0:T(32,128)(4,1)}, u32[]{:S(2)}) copy-start(pred[128,144]{1,0:T(32,128)(4,1)} %iota_compare_fusion.2) | copy-start | bytes 55300
  244.1 11.3 %copy-start.1 = (bf16[60,4096]{1,0:T(8,128)(2,1)S(1)}, bf16[60,4096]{1,0:T(8,128)(2,1)}, u32[]{:S(2)}) copy-start(bf16[60,4096]{1,0:T(8,128)(2,1)} %param.16) | copy-start | bytes 1474564
  244.1 11.3 %copy-start.4 = (bf16[4,4096]{1,0:T(4,128)(2,1)S(1)}, bf16[4,4096]{1,0:T(4,128)(2,1)}, u32[]{:S(2)}) copy-start(bf16[4,4096]{1,0:T(4,128)(2,1)} %copy-done.3) | copy-start | bytes 98308
  255.6 0.8 copy-start.2

commit v3 on v2

--- a/solution.py
+++ b/solution.py
@@ -94,72 +94,11 @@
     )
 
 
-def plane_kernel(per_half, n_expert, src_ref, dst_ref, send_sem, recv_sem, own_sem):
-    expert = lax.axis_index("expert")
-    shard = lax.axis_index("shard")
-    half, rest = shard // SHARD_PLANE, shard % SHARD_PLANE
-    mine = half * n_expert + expert
-
-    def peer(step):
-        to_expert = (expert + step % n_expert) % n_expert
-        to_half = (half + step // n_expert) % Z_HALVES
-        return to_expert, to_half
-
-    peers = Z_HALVES * n_expert
-    barrier = pltpu.get_barrier_semaphore()
-    for step in range(1, peers):
-        to_expert, to_half = peer(step)
-        pl.semaphore_signal(
-            barrier, inc=1, device_id=(to_expert, to_half * SHARD_PLANE + rest), device_id_type=MESH
-        )
-    pl.semaphore_wait(barrier, peers - 1)
-    copies = []
-    for step in range(1, peers):
-        to_expert, to_half = peer(step)
-        block = to_half * n_expert + to_expert if per_half else to_expert
-        copy = pltpu.make_async_remote_copy(
-            src_ref=src_ref.at[block],
-            dst_ref=dst_ref.at[mine],
-            send_sem=send_sem.at[step],
-            recv_sem=recv_sem.at[step],
-            device_id=(to_expert, to_half * SHARD_PLANE + rest),
-            device_id_type=MESH,
-        )
-        copy.start()
-        copies.append(copy)
-    own = pltpu.make_async_copy(src_ref.at[mine if per_half else expert], dst_ref.at[mine], own_sem)
-    own.start()
-    own.wait()
-    for copy in copies:
-        copy.wait()
-
-
-def plane_exchange(blocks, n_expert, per_half, collective_id):
-    peers = Z_HALVES * n_expert
-    block = blocks.shape[1:]
-
-    def kernel(*refs):
-        plane_kernel(per_half, n_expert, *refs)
-
-    return pl.pallas_call(
-        kernel,
-        out_shape=jax.ShapeDtypeStruct((peers,) + block, blocks.dtype),
-        in_specs=[pl.BlockSpec(memory_space=pl.ANY)],
-        out_specs=pl.BlockSpec(memory_space=pl.ANY),
-        scratch_shapes=[
-            pltpu.SemaphoreType.DMA((peers,)),
-            pltpu.SemaphoreType.DMA((peers,)),
-            pltpu.SemaphoreType.DMA,
-        ],
-        compiler_params=pltpu.CompilerParams(collective_id=collective_id, has_side_effects=True),
-        name="plane_return" if per_half else "plane_send",
-    )(blocks)
-
-
 def expert_kernel(
     blocks_ref, rest_ref, gate0, gate1, up0, up1, down0, down1, back_ref, rest_out,
-    rows, held, partial, direct, relayed, sums, act, gate, up, down,
-    plane_send, plane_recv, back_send, back_recv, send_sem, recv_sem, load_sem,
+    rows, held, partial, direct, relayed, sums, act, gate, up, down, rest_in, rest_sums, unpacked,
+    plane_send, plane_recv, back_send, back_recv, rest_send, rest_recv, over_send, over_recv,
+    send_sem, recv_sem, load_sem,
 ):
     expert = lax.axis_index("expert")
     shard = lax.axis_index("shard")
@@ -192,10 +131,7 @@
         return copy
 
     own = local_copy(6, blocks_ref.at[expert], rows.at[lines_of(0)])
-    rests = [
-        local_copy(7 + side, rest_ref.at[pl.ds(side * block, block)], rows.at[pl.ds(side * part + main, block)])
-        for side in range(2)
-    ]
+    own_rest = local_copy(7, rest_ref.at[expert], rest_in.at[0])
     loads = [
         local_copy(at, src, dst)
         for at, (src, dst) in enumerate(
@@ -210,6 +146,19 @@
         pl.semaphore_signal(barrier, inc=1, device_id=ahead(step), device_id_type=MESH)
     pl.semaphore_wait(barrier, peers + 1)
 
+    over = rest_ref.shape[1]
+    spread_rest = []
+    for step in range(1, peers):
+        copy = pltpu.make_async_remote_copy(
+            src_ref=rest_ref.at[ahead(step)[0]],
+            dst_ref=rest_in.at[step],
+            send_sem=rest_send.at[step],
+            recv_sem=rest_recv.at[step],
+            device_id=ahead(step),
+            device_id_type=MESH,
+        )
+        copy.start()
+        spread_rest.append(copy)
     spread = []
     for step in range(1, peers):
         copy = pltpu.make_async_remote_copy(
@@ -246,14 +195,20 @@
         near[side].append(send(rows.at[lines], held.at[side, lines], right))
         later.append(send(rows.at[lines], held.at[1 - side, lines], left))
 
-    for side in range(2):
-        rests[side].wait()
-        forward(pl.ds(side * part + main, block), side)
     own.wait()
     forward(lines_of(0), 0)
     for step in range(1, peers):
         spread[step - 1].wait_recv()
         forward(lines_of(step), step // n_expert)
+        if step == n_expert // 2:
+            own_rest.wait()
+            for copy in spread_rest:
+                copy.wait_recv()
+            for at in range(peers):
+                unpacked[pl.ds(at * over, over), :] = rest_in[at].astype(jnp.float32)
+            for side in range(2):
+                rows[pl.ds(side * part + main, block), :] = unpacked[pl.ds(side * block, block), :].astype(rows.dtype)
+                forward(pl.ds(side * part + main, block), side)
     for load in loads:
         load.wait()
 
@@ -340,9 +295,23 @@
             for side in range(2):
                 step = side * n_expert + at
                 if at == n_expert:
-                    locals_.append(
-                        local_copy(7 + side, sums.at[pl.ds(side * part + main, block)], rest_out.at[pl.ds(side * block, block)])
-                    )
+                    unpacked[pl.ds(side * block, block), :] = sums[pl.ds(side * part + main, block), :].astype(jnp.float32)
+                    for step in range(side * n_expert, (side + 1) * n_expert):
+                        rest_sums[step] = unpacked[pl.ds(step * over, over), :].astype(rest_sums.dtype)
+                    for step in range(side * n_expert, (side + 1) * n_expert):
+                        if step == 0:
+                            locals_.append(local_copy(7, rest_sums.at[0], rest_out.at[mine]))
+                            continue
+                        copy = pltpu.make_async_remote_copy(
+                            src_ref=rest_sums.at[step],
+                            dst_ref=rest_out.at[mine],
+                            send_sem=over_send.at[step],
+                            recv_sem=over_recv.at[step],
+                            device_id=behind(step),
+                            device_id_type=MESH,
+                        )
+                        copy.start()
+                        returns.append(copy)
                 elif step == 0:
                     locals_.append(local_copy(6, sums.at[lines_of(0)], back_ref.at[mine]))
                 else:
@@ -360,7 +329,7 @@
         copy.wait()
     for copy in returns:
         copy.wait()
-    for copy in spread + sent:
+    for copy in spread_rest + spread + sent:
         copy.wait_send()
 
 
@@ -369,14 +338,15 @@
     peers = Z_HALVES * n_expert
     ff = gates[0].shape[1]
     bf16 = jnp.bfloat16
-    count = peers * block + rest.shape[0]
+    over = rest.shape[1]
+    count = peers * (block + over)
     anywhere = pl.BlockSpec(memory_space=pl.ANY)
     sends = 2 * (peers + 2) + 8 * CHUNKS
     return pl.pallas_call(
         expert_kernel,
         out_shape=(
             jax.ShapeDtypeStruct((peers, block, width), bf16),
-            jax.ShapeDtypeStruct(rest.shape, bf16),
+            jax.ShapeDtypeStruct((peers, over, width), bf16),
         ),
         in_specs=[anywhere] * 8,
         out_specs=(anywhere, anywhere),
@@ -391,13 +361,20 @@
             pltpu.VMEM((2, width, ff), bf16),
             pltpu.VMEM((2, width, ff), bf16),
             pltpu.VMEM((2, ff, width), bf16),
+            pltpu.VMEM((peers, over, width), bf16),
+            pltpu.VMEM((peers, over, width), bf16),
+            pltpu.VMEM((peers * over, width), jnp.float32),
+            pltpu.SemaphoreType.DMA((peers,)),
+            pltpu.SemaphoreType.DMA((peers,)),
+            pltpu.SemaphoreType.DMA((peers,)),
+            pltpu.SemaphoreType.DMA((peers,)),
             pltpu.SemaphoreType.DMA((peers,)),
             pltpu.SemaphoreType.DMA((peers,)),
             pltpu.SemaphoreType.DMA((peers,)),
             pltpu.SemaphoreType.DMA((peers,)),
             pltpu.SemaphoreType.DMA((sends,)),
             pltpu.SemaphoreType.DMA((sends,)),
-            pltpu.SemaphoreType.DMA((9,)),
+            pltpu.SemaphoreType.DMA((8,)),
         ],
         compiler_params=pltpu.CompilerParams(
             collective_id=collective_id, has_side_effects=True, vmem_limit_bytes=66 * 1024 * 1000 - 560000
@@ -467,18 +444,12 @@
     ).reshape(rows_dev, 2)
     chosen = jnp.arange(slots_all, dtype=jnp.int32)[:, None, None] == slot_pos[None]
     placing = jnp.any(chosen, axis=-1).astype(jnp.bfloat16)
-    lanes = 128
     blocks = jnp.dot(placing[:main_all], normed, preferred_element_type=jnp.float32).astype(jnp.bfloat16)
     rest = jnp.dot(placing[main_all:], normed, preferred_element_type=jnp.float32).astype(jnp.bfloat16)
-    rest_in = plane_exchange(
-        rest.reshape(experts, rest_cap, width // lanes, lanes), n_expert, False, 0
-    ).reshape(-1, width)
-    back, rest_sums = expert_exchange(
-        blocks.reshape(experts, BLOCK, width), rest_in, gates, ups, downs, 1
-    )
-    rest_back = plane_exchange(
-        rest_sums.reshape(Z_HALVES * n_expert, rest_cap, width // lanes, lanes), n_expert, True, 2
-    ).reshape(Z_HALVES, experts * rest_cap, width)
+    back, rest_back = expert_exchange(
+        blocks.reshape(experts, BLOCK, width), rest.reshape(experts, rest_cap, width), gates, ups, downs, 0
+    )
+    rest_back = rest_back.reshape(Z_HALVES, experts * rest_cap, width)
     back = back.reshape(Z_HALVES, main_all, width)
     picking = (slot_pos.T.reshape(-1)[:, None] == jnp.arange(slots_all, dtype=jnp.int32)[None, :]).astype(
         jnp.bfloat16

time: 257 us -> 245 us (0.953)
  Pallas kernels: 216 us -> 206 us
  local copies, waits for them, and re-layouts: 10.6 us -> 7.24 us
    pallas_call x2 -> x0, Pallas kernels: 20 us -> none  [plane_exchange(): pl.pallas_call(kernel, out_shape=jax.ShapeDtypeStruct((peers,) + block, b...]
    pallas_call x1, Pallas kernels: 179 us -> 189 us  [expert_exchange(): pl.pallas_call(expert_kernel, out_shape=(jax.ShapeDtypeStruct((peers, blo...]
    unnamed x29 -> x26, local copies, waits for them, and re-layouts: 4.29 us -> 0.15 us
  transfers between devices with their start and end apart: 4 -> 4, of which waited for: 1 -> 1; matrix products, arithmetic and copies ran while one was open for 8% -> 8% of each run, Pallas kernels for 11% -> 7%
where the time goes in v3:
time: 245 us; the launch traced here: 244 us
  Pallas kernels  206 us (84%)
  other arithmetic  11.6 us (5%)
  local copies, waits for them, and re-layouts  7.24 us (3%)
  starting transfers between devices  6.59 us (3%)
  matrix products  6.38 us (3%)
  waiting for transfers between devices  5.31 us (2%)
    pallas_call x1, Pallas kernels, expert_exchange(): pl.pallas_call(expert_kernel, out_shape=(jax.ShapeDtypeStruct((peers, blo...  189 us
    pallas_call x1, Pallas kernels, pool_attention(): pl.pallas_call(attention_kernel, grid=(steps,), in_specs=[pl.BlockSpec((r...  16.9 us
    all_to_all x1, starting transfers between devices, local(): lax.all_to_all(head_part.reshape(n_expert, -1, head_part.shape[1]), 'expe...  5.91 us
    reduce_sum x1, other arithmetic, pool_attention(): jnp.sum(jnp.where(page_rows[:, :, None] == pool_ids[None, None, :], in_pa...  5.66 us
    all_to_all x1, waiting for transfers between devices, local(): lax.all_to_all(head_part.reshape(n_expert, -1, head_part.shape[1]), 'expe...  5.3 us
  transfers between devices with their start and end apart: 4, of which 1 were waited for; matrix products, arithmetic and copies ran while one was open for 8% of the time, Pallas kernels for 7%

profile of v3, /device:TPU:0, one launch (start us, length us, event | category | flops | bytes accessed | tf_op | source)
XLA Modules:
  0.0 243.8 jit_solution(17726712713143198937)
XLA Ops:
  0.7 0.5 collective-permute-start.1
  1.2 0.1 collective-permute-start.2
  1.3 0.7 subtract_clamp_fusion
  2.0 5.7 %select_reduce_fusion = s32[32,1056]{1,0:T(8,128)S(1)} fusion(s32[32,128]{1,0:T(8,128)S(1)} %subtract_clamp_fusion, s32[32,128]{1,0:T(8,128)} %bitcast.39), kind=kLoop, calls=%fused_computation | loop fusion | flops 12942336 | bytes 167936 | tf_op jit(solution)/shard_map/reduce_sum | solution.py:66
  7.8 0.9 reshape_reshape.3
  8.8 0.9 copy.29
  9.7 1.4 reshape.121.q_ref
  11.1 16.9 %pool_attention.1 = bf16[128,128]{1,0:T(8,128)(2,1)} custom-call(bf16[128,128]{1,0:T(8,128)(2,1)} %reshape.121.q_ref, bf16[16,128,66]{2,1,0:T(8,128)(2,1)} %bitcast.37, bf16[16896,256]{1,0:T(8,128)(2,1)} %bitcast.28), custom_call_target="tpu_custom_call" | custom-call | flops 1107296256 | bytes 8650752 | tf_op jit(solution)/shard_map/pool_attention/pallas_call | solution.py:71
  28.1 0.8 reshape.123
  28.9 3.0 %convolution_convert_fusion.1 = bf16[32,4096]{1,0:T(8,128)(2,1)S(1)} fusion(bf16[32,512]{1,0:T(8,128)(2,1)S(1)} %reshape.123, bf16[512,4096]{1,0:T(8,128)(2,1)} %param.22), kind=kOutput, calls=%fused_computation.4 | convolution fusion | flops 134348800 | bytes 4489216 | tf_op jit(solution)/shard_map/dot_general | solution.py:411
  31.9 0.8 reshape.124
  32.7 5.9 %all-to-all-start = ((bf16[8,4,4096]{2,1,0:T(4,128)(2,1)}), bf16[8,4,4096]{2,1,0:T(4,128)(2,1)S(1)}, u32[]{:S(2)}, u32[]{:S(2)}) async-start(bf16[8,4,4096]{2,1,0:T(4,128)(2,1)} %reshape.124), calls=%async_computation | async-start | bytes 524288 | tf_op jit(solution)/shard_map/all_to_all | solution.py:412
  38.8 0.1 select_reduce_fusion.3
  39.0 0.1 copy.24
  39.1 0.1 eq.94
  39.3 0.2 reduce_window_sum.11
  39.5 0.2 select_reduce_fusion.1
  39.6 0.1 reduce_sum.61
  40.2 0.7 iota_compare_fusion.2
  40.9 5.3 %all-to-all-done = bf16[8,4,4096]{2,1,0:T(4,128)(2,1)S(1)} async-done(((bf16[8,4,4096]{2,1,0:T(4,128)(2,1)}), bf16[8,4,4096]{2,1,0:T(4,128)(2,1)S(1)}, u32[]{:S(2)}, u32[]{:S(2)}) %all-to-all-start) | async-done | bytes 262176 | tf_op jit(solution)/shard_map/all_to_all | solution.py:412
  46.2 0.1 convert_reduce_fusion
  46.3 0.2 fusion
  46.6 0.3 convolution_convert_fusion.2
  46.9 0.8 reshape.126.rest_ref
  47.7 1.5 convolution_convert_fusion
  49.2 188.8 %expert_exchange.1 = (bf16[16,16,4096]{2,1,0:T(8,128)(2,1)}, bf16[16,2,4096]{2,1,0:T(2,128)(2,1)}) custom-call(bf16[8,16,4096]{2,1,0:T(8,128)(2,1)} %bitcast.36, bf16[8,2,4096]{2,1,0:T(2,128)(2,1)} %reshape.126.rest_ref, bf16[4096,512]{1,0:T(8,128)(2,1)} %bitcast.30, bf16[4096,512]{1,0:T(8,128)(2,1)} %collective-permute-done.gate1, ...), custom_call_target="tpu_custom_call" | custom-call | tf_op jit(solution)/shard_map/expert_exchange/pallas_call | solution.py:345
  238.0 1.8 add_convert_fusion
  239.9 1.2 add_convert_fusion.1
  241.1 1.2 fusion.11
  242.3 0.4 convolution_add_fusion
  242.7 0.3 fusion.4
  243.0 0.7 slice_bitcast_fusion
  (45 shorter events, 1.0 us)
Async XLA Ops:
  0.6 48.5 %collective-permute-start = (bf16[4096,512]{1,0:T(8,128)(2,1)}, bf16[4096,512]{1,0:T(8,128)(2,1)}, u32[]{:S(2)}, u32[]{:S(2)}) collective-permute-start(bf16[4096,512]{1,0:T(8,128)(2,1)} %bitcast.29), channel_id=1, source_target_pairs={{0,1},{1,0},{2,3},{3,2},{4,5},{5,4},{6,7},{7,6},{8,9},{9,8},{10,11... | collective-permute-start | bytes 12582920 | tf_op jit(solution)/shard_map/ppermute | solution.py:407
  0.7 48.4 %collective-permute-start.1 = (bf16[4096,512]{1,0:T(8,128)(2,1)}, bf16[4096,512]{1,0:T(8,128)(2,1)}, u32[]{:S(2)}, u32[]{:S(2)}) collective-permute-start(bf16[4096,512]{1,0:T(8,128)(2,1)} %bitcast.31), channel_id=1, source_target_pairs={{0,1},{1,0},{2,3},{3,2},{4,5},{5,4},{6,7},{7,6},{8,9},{9,8},{10,11... | collective-permute-start | bytes 12582920 | tf_op jit(solution)/shard_map/ppermute | solution.py:408
  1.2 48.0 %collective-permute-start.2 = (bf16[512,4096]{1,0:T(8,128)(2,1)}, bf16[512,4096]{1,0:T(8,128)(2,1)}, u32[]{:S(2)}, u32[]{:S(2)}) collective-permute-start(bf16[512,4096]{1,0:T(8,128)(2,1)} %bitcast.33), channel_id=1, source_target_pairs={{0,1},{1,0},{2,3},{3,2},{4,5},{5,4},{6,7},{7,6},{8,9},{9,8},{10,11... | collective-permute-start | bytes 12582920 | tf_op jit(solution)/shard_map/ppermute | solution.py:409
  28.0 10.7 %copy-start.8 = (s32[1,4,2]{1,2,0:T(2,128)S(1)}, s32[1,4,2]{1,2,0:T(2,128)}, u32[]{:S(2)}) copy-start(s32[1,4,2]{1,2,0:T(2,128)} %param.25) | copy-start | bytes 100
  28.0 10.7 %copy-start.9 = (s32[60,2]{0,1:T(2,128)S(1)}, s32[60,2]{0,1:T(2,128)}, u32[]{:S(2)}) copy-start(s32[60,2]{0,1:T(2,128)} %param.24) | copy-start | bytes 1444
  28.0 10.7 %copy-start.12 = (s32[8]{0:T(128)S(1)}, s32[8]{0:T(128)}, u32[]{:S(2)}) copy-start(s32[8]{0:T(128)} %param.28) | copy-start | bytes 100
  28.0 11.9 %copy-start.10 = (f32[1,4,2]{1,2,0:T(2,128)S(1)}, f32[1,4,2]{1,2,0:T(2,128)}, u32[]{:S(2)}) copy-start(f32[1,4,2]{1,2,0:T(2,128)} %param.27) | copy-start | bytes 100
  28.0 11.8 %copy-start.11 = (f32[60,2]{0,1:T(2,128)S(1)}, f32[60,2]{0,1:T(2,128)}, u32[]{:S(2)}) copy-start(f32[60,2]{0,1:T(2,128)} %param.26) | copy-start | bytes 1444
  28.0 18.3 %copy-start.6 = (bf16[1,4,4096]{2,1,0:T(4,128)(2,1)S(1)}, bf16[1,4,4096]{2,1,0:T(4,128)(2,1)}, u32[]{:S(2)}) copy-start(bf16[1,4,4096]{2,1,0:T(4,128)(2,1)} %param.17) | copy-start | bytes 98308
  28.0 18.3 %copy-start = (bf16[60,4096]{1,0:T(8,128)(2,1)S(1)}, bf16[60,4096]{1,0:T(8,128)(2,1)}, u32[]{:S(2)}) copy-start(bf16[60,4096]{1,0:T(8,128)(2,1)} %param.16) | copy-start | bytes 1474564
  28.1 18.5 %copy-start.7 = (f32[4096]{0:T(1024)S(1)}, f32[4096]{0:T(1024)}, u32[]{:S(2)}) copy-start(f32[4096]{0:T(1024)} %param.23) | copy-start | bytes 49156
  32.7 13.4 %all-to-all-start = ((bf16[8,4,4096]{2,1,0:T(4,128)(2,1)}), bf16[8,4,4096]{2,1,0:T(4,128)(2,1)S(1)}, u32[]{:S(2)}, u32[]{:S(2)}) async-start(bf16[8,4,4096]{2,1,0:T(4,128)(2,1)} %reshape.124), calls=%async_computation | async-start | bytes 524288 | tf_op jit(solution)/shard_map/all_to_all | solution.py:412
  46.3 2.8 %copy-start.3 = (bf16[4,4096]{1,0:T(4,128)(2,1)}, bf16[4,4096]{1,0:T(4,128)(2,1)S(1)}, u32[]{:S(2)}) copy-start(bf16[4,4096]{1,0:T(4,128)(2,1)S(1)} %fusion.8) | copy-start | bytes 98308
  238.0 4.2 %copy-start.5 = (pred[128,144]{1,0:T(32,128)(4,1)S(1)}, pred[128,144]{1,0:T(32,128)(4,1)}, u32[]{:S(2)}) copy-start(pred[128,144]{1,0:T(32,128)(4,1)} %iota_compare_fusion.2) | copy-start | bytes 55300
  239.8 2.9 %copy-start.1 = (bf16[60,4096]{1,0:T(8,128)(2,1)S(1)}, bf16[60,4096]{1,0:T(8,128)(2,1)}, u32[]{:S(2)}) copy-start(bf16[60,4096]{1,0:T(8,128)(2,1)} %param.16) | copy-start | bytes 1474564
  239.8 2.9 %copy-start.4 = (bf16[4,4096]{1,0:T(4,128)(2,1)S(1)}, bf16[4,4096]{1,0:T(4,128)(2,1)}, u32[]{:S(2)}) copy-start(bf16[4,4096]{1,0:T(4,128)(2,1)} %copy-done.3) | copy-start | bytes 98308
  243.0 0.8 copy-start.2

commit v4 on v3

--- a/solution.py
+++ b/solution.py
@@ -15,27 +15,26 @@
 CHUNKS = 3
 
 
-def attention_kernel(q_ref, count_ref, kv_ref, out_ref, top, total, summed):
+def attention_kernel(q_ref, count_ref, kv_ref, out_ref, top, total, summed, spread, offset):
     step = pl.program_id(0)
+    head_dim = q_ref.shape[1]
+    pages, positions = spread.shape
+    page_size = positions // pages
 
     @pl.when(step == 0)
     def _():
         top[...] = jnp.full(top.shape, LOWEST, jnp.float32)
         total[...] = jnp.zeros(total.shape, jnp.float32)
         summed[...] = jnp.zeros(summed.shape, jnp.float32)
-
-    head_dim = q_ref.shape[1]
-    positions = kv_ref.shape[0]
-    pages = count_ref.shape[2]
-    page_size = positions // pages
+        page_of = lax.broadcasted_iota(jnp.int32, (pages, positions), 1) // page_size
+        spread[...] = (page_of == lax.broadcasted_iota(jnp.int32, (pages, positions), 0)).astype(spread.dtype)
+        offset[...] = (lax.broadcasted_iota(jnp.int32, (1, positions), 1) % page_size).astype(jnp.float32)
+
     scores = lax.dot_general(
         q_ref[...], kv_ref[:, :head_dim], (((1,), (1,)), ((), ())), preferred_element_type=jnp.float32
     ) * head_dim ** (-0.5)
-    page_of = lax.broadcasted_iota(jnp.int32, (pages, positions), 1) // page_size
-    spread = (page_of == lax.broadcasted_iota(jnp.int32, (pages, positions), 0)).astype(jnp.bfloat16)
-    counts = jnp.dot(count_ref[0], spread, preferred_element_type=jnp.float32)
-    offset = (lax.broadcasted_iota(jnp.int32, (1, positions), 1) % page_size).astype(jnp.float32)
-    live = counts > offset
+    counts = jnp.dot(count_ref[0], spread[...], preferred_element_type=jnp.float32)
+    live = counts > offset[...]
     scores = jnp.where(live, scores, LOWEST)
     new_top = jnp.maximum(top[...], jnp.max(scores, axis=1, keepdims=True))
     scale = jnp.exp(top[...] - new_top)
@@ -57,7 +56,7 @@
     head_dim = twice_dim // 2
     group = local_cols // head_dim
     max_pages = page_rows.shape[1]
-    steps = 16
+    steps = 6
     pages = pool_dev // steps
     in_page = jnp.clip(
         lengths[:, None] - page_size * jnp.arange(max_pages, dtype=jnp.int32)[None, :], 0, page_size
@@ -82,6 +81,8 @@
             pltpu.VMEM((rows, 1), jnp.float32),
             pltpu.VMEM((rows, 1), jnp.float32),
             pltpu.VMEM((rows, head_dim), jnp.float32),
+            pltpu.VMEM((pages, pages * page_size), jnp.bfloat16),
+            pltpu.VMEM((1, pages * page_size), jnp.float32),
         ],
         cost_estimate=pl.CostEstimate(
             flops=4 * rows * head_dim * pool_dev * page_size,

time: 245 us -> 238 us (0.971)
  Pallas kernels: 206 us -> 200 us
    pallas_call x1, Pallas kernels: 16.9 us -> 10.9 us  [pool_attention(): pl.pallas_call(attention_kernel, grid=(steps,), in_specs=[pl.BlockSpec((r...]
  transfers between devices with their start and end apart: 4 -> 4, of which waited for: 1 -> 1; matrix products, arithmetic and copies ran while one was open for 8% -> 8% of each run, Pallas kernels for 7% -> 5%
where the time goes in v4:
time: 238 us; the launch traced here: 237 us
  Pallas kernels  200 us (84%)
  other arithmetic  11.6 us (5%)
  local copies, waits for them, and re-layouts  6.81 us (3%)
  starting transfers between devices  6.59 us (3%)
  matrix products  6.38 us (3%)
  waiting for transfers between devices  5.31 us (2%)
    pallas_call x1, Pallas kernels, expert_exchange(): pl.pallas_call(expert_kernel, out_shape=(jax.ShapeDtypeStruct((peers, blo...  189 us
    pallas_call x1, Pallas kernels, pool_attention(): pl.pallas_call(attention_kernel, grid=(steps,), in_specs=[pl.BlockSpec((r...  10.9 us
    all_to_all x1, starting transfers between devices, local(): lax.all_to_all(head_part.reshape(n_expert, -1, head_part.shape[1]), 'expe...  5.91 us
    reduce_sum x1, other arithmetic, pool_attention(): jnp.sum(jnp.where(page_rows[:, :, None] == pool_ids[None, None, :], in_pa...  5.66 us
    all_to_all x1, waiting for transfers between devices, local(): lax.all_to_all(head_part.reshape(n_expert, -1, head_part.shape[1]), 'expe...  5.3 us
  transfers between devices with their start and end apart: 4, of which 1 were waited for; matrix products, arithmetic and copies ran while one was open for 8% of the time, Pallas kernels for 5%

profile of v4, /device:TPU:0, one launch (start us, length us, event | category | flops | bytes accessed | tf_op | source)
XLA Modules:
  0.0 237.4 jit_solution(1476200196027064967)
XLA Ops:
  0.7 0.5 collective-permute-start.1
  1.2 0.1 collective-permute-start.2
  1.3 0.7 subtract_clamp_fusion
  2.0 5.7 %select_reduce_fusion = s32[32,1056]{1,0:T(8,128)S(1)} fusion(s32[32,128]{1,0:T(8,128)S(1)} %subtract_clamp_fusion, s32[32,128]{1,0:T(8,128)} %bitcast.39), kind=kLoop, calls=%fused_computation | loop fusion | flops 12942336 | bytes 167936 | tf_op jit(solution)/shard_map/reduce_sum | solution.py:65
  7.8 0.6 reshape_reshape.3
  8.4 0.8 copy.29
  9.3 1.4 reshape.121.q_ref
  10.7 10.9 %pool_attention.1 = bf16[128,128]{1,0:T(8,128)(2,1)} custom-call(bf16[128,128]{1,0:T(8,128)(2,1)} %reshape.121.q_ref, bf16[6,128,176]{2,1,0:T(8,128)(2,1)} %bitcast.37, bf16[16896,256]{1,0:T(8,128)(2,1)} %bitcast.28), custom_call_target="tpu_custom_call" | custom-call | flops 1107296256 | bytes 8650752 | tf_op jit(solution)/shard_map/pool_attention/pallas_call | solution.py:70
  21.6 0.8 reshape.123
  22.5 3.0 %convolution_convert_fusion.1 = bf16[32,4096]{1,0:T(8,128)(2,1)S(1)} fusion(bf16[32,512]{1,0:T(8,128)(2,1)S(1)} %reshape.123, bf16[512,4096]{1,0:T(8,128)(2,1)} %param.22), kind=kOutput, calls=%fused_computation.4 | convolution fusion | flops 134348800 | bytes 4489216 | tf_op jit(solution)/shard_map/dot_general | solution.py:412
  25.5 0.8 reshape.124
  26.3 5.9 %all-to-all-start = ((bf16[8,4,4096]{2,1,0:T(4,128)(2,1)}), bf16[8,4,4096]{2,1,0:T(4,128)(2,1)S(1)}, u32[]{:S(2)}, u32[]{:S(2)}) async-start(bf16[8,4,4096]{2,1,0:T(4,128)(2,1)} %reshape.124), calls=%async_computation | async-start | bytes 524288 | tf_op jit(solution)/shard_map/all_to_all | solution.py:413
  32.3 0.1 select_reduce_fusion.3
  32.5 0.1 copy.24
  32.6 0.1 eq.94
  32.9 0.2 reduce_window_sum.11
  33.0 0.2 select_reduce_fusion.1
  33.2 0.1 reduce_sum.61
  33.7 0.7 iota_compare_fusion.2
  34.4 5.3 %all-to-all-done = bf16[8,4,4096]{2,1,0:T(4,128)(2,1)S(1)} async-done(((bf16[8,4,4096]{2,1,0:T(4,128)(2,1)}), bf16[8,4,4096]{2,1,0:T(4,128)(2,1)S(1)}, u32[]{:S(2)}, u32[]{:S(2)}) %all-to-all-start) | async-done | bytes 262176 | tf_op jit(solution)/shard_map/all_to_all | solution.py:413
  39.7 0.1 convert_reduce_fusion
  39.9 0.2 fusion
  40.2 0.3 convolution_convert_fusion.2
  40.5 0.8 reshape.126.rest_ref
  41.2 1.5 convolution_convert_fusion
  42.8 188.8 %expert_exchange.1 = (bf16[16,16,4096]{2,1,0:T(8,128)(2,1)}, bf16[16,2,4096]{2,1,0:T(2,128)(2,1)}) custom-call(bf16[8,16,4096]{2,1,0:T(8,128)(2,1)} %bitcast.36, bf16[8,2,4096]{2,1,0:T(2,128)(2,1)} %reshape.126.rest_ref, bf16[4096,512]{1,0:T(8,128)(2,1)} %bitcast.30, bf16[4096,512]{1,0:T(8,128)(2,1)} %collective-permute-done.gate1, ...), custom_call_target="tpu_custom_call" | custom-call | tf_op jit(solution)/shard_map/expert_exchange/pallas_call | solution.py:346
  231.6 1.8 add_convert_fusion
  233.4 1.2 add_convert_fusion.1
  234.6 1.2 fusion.11
  235.8 0.4 convolution_add_fusion
  236.3 0.3 fusion.4
  236.6 0.7 slice_bitcast_fusion
  (45 shorter events, 1.0 us)
Async XLA Ops:
  0.6 42.1 %collective-permute-start = (bf16[4096,512]{1,0:T(8,128)(2,1)}, bf16[4096,512]{1,0:T(8,128)(2,1)}, u32[]{:S(2)}, u32[]{:S(2)}) collective-permute-start(bf16[4096,512]{1,0:T(8,128)(2,1)} %bitcast.29), channel_id=1, source_target_pairs={{0,1},{1,0},{2,3},{3,2},{4,5},{5,4},{6,7},{7,6},{8,9},{9,8},{10,11... | collective-permute-start | bytes 12582920 | tf_op jit(solution)/shard_map/ppermute | solution.py:408
  0.7 42.0 %collective-permute-start.1 = (bf16[4096,512]{1,0:T(8,128)(2,1)}, bf16[4096,512]{1,0:T(8,128)(2,1)}, u32[]{:S(2)}, u32[]{:S(2)}) collective-permute-start(bf16[4096,512]{1,0:T(8,128)(2,1)} %bitcast.31), channel_id=1, source_target_pairs={{0,1},{1,0},{2,3},{3,2},{4,5},{5,4},{6,7},{7,6},{8,9},{9,8},{10,11... | collective-permute-start | bytes 12582920 | tf_op jit(solution)/shard_map/ppermute | solution.py:409
  1.2 41.5 %collective-permute-start.2 = (bf16[512,4096]{1,0:T(8,128)(2,1)}, bf16[512,4096]{1,0:T(8,128)(2,1)}, u32[]{:S(2)}, u32[]{:S(2)}) collective-permute-start(bf16[512,4096]{1,0:T(8,128)(2,1)} %bitcast.33), channel_id=1, source_target_pairs={{0,1},{1,0},{2,3},{3,2},{4,5},{5,4},{6,7},{7,6},{8,9},{9,8},{10,11... | collective-permute-start | bytes 12582920 | tf_op jit(solution)/shard_map/ppermute | solution.py:410
  21.6 10.7 %copy-start.8 = (s32[1,4,2]{1,2,0:T(2,128)S(1)}, s32[1,4,2]{1,2,0:T(2,128)}, u32[]{:S(2)}) copy-start(s32[1,4,2]{1,2,0:T(2,128)} %param.25) | copy-start | bytes 100
  21.6 10.7 %copy-start.9 = (s32[60,2]{0,1:T(2,128)S(1)}, s32[60,2]{0,1:T(2,128)}, u32[]{:S(2)}) copy-start(s32[60,2]{0,1:T(2,128)} %param.24) | copy-start | bytes 1444
  21.6 10.7 %copy-start.12 = (s32[8]{0:T(128)S(1)}, s32[8]{0:T(128)}, u32[]{:S(2)}) copy-start(s32[8]{0:T(128)} %param.28) | copy-start | bytes 100
  21.6 11.9 %copy-start.10 = (f32[1,4,2]{1,2,0:T(2,128)S(1)}, f32[1,4,2]{1,2,0:T(2,128)}, u32[]{:S(2)}) copy-start(f32[1,4,2]{1,2,0:T(2,128)} %param.27) | copy-start | bytes 100
  21.6 11.8 %copy-start.11 = (f32[60,2]{0,1:T(2,128)S(1)}, f32[60,2]{0,1:T(2,128)}, u32[]{:S(2)}) copy-start(f32[60,2]{0,1:T(2,128)} %param.26) | copy-start | bytes 1444
  21.6 18.3 %copy-start.6 = (bf16[1,4,4096]{2,1,0:T(4,128)(2,1)S(1)}, bf16[1,4,4096]{2,1,0:T(4,128)(2,1)}, u32[]{:S(2)}) copy-start(bf16[1,4,4096]{2,1,0:T(4,128)(2,1)} %param.17) | copy-start | bytes 98308
  21.6 18.3 %copy-start = (bf16[60,4096]{1,0:T(8,128)(2,1)S(1)}, bf16[60,4096]{1,0:T(8,128)(2,1)}, u32[]{:S(2)}) copy-start(bf16[60,4096]{1,0:T(8,128)(2,1)} %param.16) | copy-start | bytes 1474564
  21.6 18.5 %copy-start.7 = (f32[4096]{0:T(1024)S(1)}, f32[4096]{0:T(1024)}, u32[]{:S(2)}) copy-start(f32[4096]{0:T(1024)} %param.23) | copy-start | bytes 49156
  26.3 13.4 %all-to-all-start = ((bf16[8,4,4096]{2,1,0:T(4,128)(2,1)}), bf16[8,4,4096]{2,1,0:T(4,128)(2,1)S(1)}, u32[]{:S(2)}, u32[]{:S(2)}) async-start(bf16[8,4,4096]{2,1,0:T(4,128)(2,1)} %reshape.124), calls=%async_computation | async-start | bytes 524288 | tf_op jit(solution)/shard_map/all_to_all | solution.py:413
  39.9 2.8 %copy-start.3 = (bf16[4,4096]{1,0:T(4,128)(2,1)}, bf16[4,4096]{1,0:T(4,128)(2,1)S(1)}, u32[]{:S(2)}) copy-start(bf16[4,4096]{1,0:T(4,128)(2,1)S(1)} %fusion.8) | copy-start | bytes 98308
  231.6 4.2 %copy-start.5 = (pred[128,144]{1,0:T(32,128)(4,1)S(1)}, pred[128,144]{1,0:T(32,128)(4,1)}, u32[]{:S(2)}) copy-start(pred[128,144]{1,0:T(32,128)(4,1)} %iota_compare_fusion.2) | copy-start | bytes 55300
  233.4 2.9 %copy-start.1 = (bf16[60,4096]{1,0:T(8,128)(2,1)S(1)}, bf16[60,4096]{1,0:T(8,128)(2,1)}, u32[]{:S(2)}) copy-start(bf16[60,4096]{1,0:T(8,128)(2,1)} %param.16) | copy-start | bytes 1474564
  233.4 2.8 %copy-start.4 = (bf16[4,4096]{1,0:T(4,128)(2,1)S(1)}, bf16[4,4096]{1,0:T(4,128)(2,1)}, u32[]{:S(2)}) copy-start(bf16[4,4096]{1,0:T(4,128)(2,1)} %copy-done.3) | copy-start | bytes 98308
  236.6 0.8 copy-start.2
